TPU v7x, 32 devices: a whole 2x2x4 slice. The times are simulated.
32 devices in a mesh: tmpl: 2 (over y), freq: 16 (over z, x, core).
Axes of the slice: x: 2, y: 2, z: 4, core: 2. Of those that a mesh axis runs over, the one named last changes fastest.
Arguments:
- strain: bfloat16 [3, 1024, 512], P(None, 'freq'), may hold values from -6 to 6
- gate_start: int32 [3, 2], replicated, may hold values from 0 to 520191
- psd_inverse: float32 [3, 512, 1024], P(None, 'freq'), may hold values from 0.5 to 6, as said below
- templates: bfloat16 [8, 2, 512, 1024], P('tmpl', None, 'freq'), may hold values from -6 to 6
- basis: bfloat16 [3, 4, 512, 1024], P(None, None, 'freq'), may hold values from -2.5 to 4.5
Outputs:
- best: float32 [512, 1024], P('tmpl', 'freq')
Inputs may be any that keep to these rules, and one draw needn't show every extreme that they name: `psd_inverse`: positive weights.
All inputs are finite; a program needn't handle non-finite values.
Results may differ from a plain program's by a relative error of at most 0.004.
Values may be sent and summed in bfloat16 or wider, within the bound.
No kernel may reach another device: no remote copies, remote signals or barrier semaphores. Data moves between devices by JAX's collectives and lax.ppermute only.
A program may use at most 128 MiB of HBM per device.

v0:
```python
import functools
import math

import jax
import jax.numpy as jnp
from jax import lax
from jax.experimental import pallas as pl
from jax.experimental.pallas import tpu as pltpu
from jax.sharding import PartitionSpec as P


N1 = 512
N2 = 1024
DET = 3
CAL = 4
RESP = 5
GATE_LEN = 4096
MODULUS = N1 * N2
RADIX_C = 8
RADIX_R = 4
PART = 128
HALF_ROOT = math.sqrt(0.5)


def phase(products, length):
    angles = (products % length).astype(jnp.float32) * (2.0 * math.pi / length)
    return jnp.cos(angles), jnp.sin(angles)


def times(left, right):
    return left[0] * right[0] - left[1] * right[1], left[0] * right[1] + left[1] * right[0]


def product_phase(rows, cols, length):
    fine = jnp.arange(32, dtype=jnp.int32)
    coarse = 32 * jnp.arange(rows // 32, dtype=jnp.int32)
    high = phase(coarse[:, None] * cols, length)
    low = phase(fine[:, None] * cols, length)
    real, imag = times([h[:, None] for h in high], [w[None] for w in low])
    return real.reshape(rows, -1), imag.reshape(rows, -1)


def iota(count):
    return jnp.arange(count, dtype=jnp.int32)


def row_table(zero):
    cos_r, sin_r = product_phase(N1, zero + iota(N1)[None], N1)
    return jnp.concatenate([cos_r, -sin_r], axis=0).astype(jnp.bfloat16)


def block_table(real, imag, transposed):
    up, low = (-imag, imag) if transposed else (imag, -imag)
    top = jnp.concatenate([real, up], axis=2)
    return jnp.concatenate([top, jnp.concatenate([low, real], axis=2)], axis=1).astype(jnp.bfloat16)


def lag_columns(zero):
    return zero + iota(RADIX_C)[:, None] + RADIX_C * iota(PART)[None, :]


def column_tables(zero):
    cols = lag_columns(zero)
    stage_one = block_table(*phase(iota(PART)[None, :, None] * cols[:, None, :], N2), False)
    coarse = 32 * iota(N1 // 32)
    high = phase(coarse[None, :, None] * cols[:, None, :], MODULUS)
    low = phase(iota(32)[None, :, None] * cols[:, None, :], MODULUS)
    real, imag = times([h[:, :, None] for h in high], [w[:, None] for w in low])
    twiddle = jnp.concatenate([real, imag], axis=3).reshape(RADIX_C, N1, 2 * PART)
    return stage_one, twiddle


def lag_tables(zero):
    rows = zero + iota(RADIX_R)[:, None] + RADIX_R * iota(PART)[None, :]
    stage_two = block_table(*phase(rows[:, :, None] * iota(PART)[None, None, :], N1), True)
    order = lag_columns(zero).reshape(-1)
    unscramble = (order[:, None] == iota(N2)[None, :]).astype(jnp.bfloat16)
    return stage_two, unscramble


class Plan:
    def __init__(self, freq, templates, groups):
        self.freq, self.width, self.groups = freq, templates, groups
        self.planes = freq // templates
        self.bits = [1 << b for b in reversed(range(templates.bit_length() - 1))]
        self.offsets = [0]
        for b in self.bits:
            self.offsets = self.offsets + [o ^ b for o in self.offsets]

    def swap(self, bit):
        return [(f, f ^ bit) for f in range(self.freq)]

    def devices(self, pairs):
        w = self.width
        return [(a * w + k, b * w + k) for a, b in pairs for k in range(w)]

    def shift_in(self, o):
        n = self.planes
        return self.devices([(z, (z + o) % n) for z in range(n) if (z + o) % n < DET])

    def shift_out(self, o):
        n = self.planes
        return self.devices([(z, (z + o) % n) for z in range(DET)])

    def back(self):
        n = self.planes
        return self.devices([(z, (z - 1) % n) for z in range(n)])


def pick(array, index, axis=0):
    return lax.dynamic_index_in_dim(array, index, axis, keepdims=False)


def scatter_planes(plan, plane, array):
    got = [pick(array, jnp.minimum(plane, DET - 1))]
    for o in range(1, plan.planes):
        send = pick(array, jnp.minimum((plane + o) % plan.planes, DET - 1))
        got.append(lax.ppermute(send, "freq", plan.shift_in(o)))
    return jnp.stack(got)


def gather_plane(plan, piece):
    held = piece[None]
    pieces = [held]
    for b in plan.bits:
        got = lax.ppermute(held, "freq", plan.swap(b))
        pieces.append(got)
        held = jnp.concatenate([held, got])
    return pieces


def scatter_templates(plan, place, templates):
    held = templates[None]
    for b in plan.bits:
        mine = (place // b) % 2
        halves = held.reshape((held.shape[0], 2, held.shape[1] // 2) + held.shape[2:])
        got = lax.ppermute(pick(halves, 1 - mine, 1), "freq", plan.swap(b))
        held = jnp.concatenate([pick(halves, mine, 1), got])
    return held[:, 0]


def gather_templates(plan, piece):
    pieces = [piece]
    for _ in range(1, plan.planes):
        pieces.append(lax.ppermute(pieces[-1], "freq", plan.back()))
    return pieces


def dft_eight(real, imag):
    def add(a, b):
        return real_imag[a][0] + real_imag[b][0], real_imag[a][1] + real_imag[b][1]

    def sub(a, b):
        return real_imag[a][0] - real_imag[b][0], real_imag[a][1] - real_imag[b][1]

    real_imag = list(zip(real, imag))
    a0, a1 = add(0, 4), sub(0, 4)
    a2, a3 = add(2, 6), sub(2, 6)
    a4, a5 = add(1, 5), sub(1, 5)
    a6, a7 = add(3, 7), sub(3, 7)
    e0 = (a0[0] + a2[0], a0[1] + a2[1])
    e1 = (a0[0] - a2[0], a0[1] - a2[1])
    o0 = (a4[0] + a6[0], a4[1] + a6[1])
    o1 = (a4[0] - a6[0], a4[1] - a6[1])
    f0 = (a1[0] - a3[1], a1[1] + a3[0])
    f1 = (a1[0] + a3[1], a1[1] - a3[0])
    m = (HALF_ROOT * (a5[0] - a7[0]), HALF_ROOT * (a5[1] - a7[1]))
    n = (HALF_ROOT * (a5[0] + a7[0]), HALF_ROOT * (a5[1] + a7[1]))
    g0 = (m[0] - n[1], m[1] + n[0])
    g1 = (-m[0] - n[1], n[0] - m[1])
    return [
        (e0[0] + o0[0], e0[1] + o0[1]),
        (f0[0] + g0[0], f0[1] + g0[1]),
        (e1[0] - o1[1], e1[1] + o1[0]),
        (f1[0] + g1[0], f1[1] + g1[1]),
        (e0[0] - o0[0], e0[1] - o0[1]),
        (f0[0] - g0[0], f0[1] - g0[1]),
        (e1[0] + o1[1], e1[1] - o1[0]),
        (f1[0] - g1[0], f1[1] - g1[1]),
    ]


def dft_four(real, imag):
    s0, s1 = (real[0] + real[2], imag[0] + imag[2]), (real[0] - real[2], imag[0] - imag[2])
    t0, t1 = (real[1] + real[3], imag[1] + imag[3]), (real[1] - real[3], imag[1] - imag[3])
    return [
        (s0[0] + t0[0], s0[1] + t0[1]),
        (s1[0] - t1[1], s1[1] + t1[0]),
        (s0[0] - t0[0], s0[1] - t0[1]),
        (s1[0] + t1[1], s1[1] - t1[0]),
    ]


def from_plane_gather(plan, plane, place, pieces, put):
    m = 0
    for piece in pieces:
        for i in range(piece.shape[0]):
            for o in range(plan.planes):
                behind = lax.rem(plane - o + plan.planes, plan.planes)
                put(piece.at[i, o], behind * plan.width + (place ^ plan.offsets[m]))
            m += 1


def spectrum_kernel(plan, rows, where_ref, gates_ref, row_table_ref, stage_one, twiddle, *rest):
    pieces, rest = rest[: 1 + len(plan.bits)], rest[1 + len(plan.bits) :]
    out, blocks, samples, parts, sem = rest
    plane, place = where_ref[0], where_ref[1]

    @pl.when(plane < DET)
    def _():
        from_plane_gather(
            plan,
            plane,
            place,
            pieces,
            lambda src, f: pltpu.make_async_copy(src, blocks.at[f], sem).start(),
        )
        pltpu.make_async_copy(blocks, blocks, sem).wait()
        tiles = N1 // PART

        starts = [gates_ref[plane, g] for g in range(gates_ref.shape[1])]
        step = lax.broadcasted_iota(jnp.int32, (rows, PART), 0)
        step = step + N2 * lax.broadcasted_iota(jnp.int32, (rows, PART), 1)

        def spread(block, carry):
            piece = blocks[block, 0].astype(jnp.float32)
            for half in range(2):
                at = pl.ds(pl.multiple_of((2 * block + half) * rows, rows), rows)
                for t in range(tiles):
                    first = half * N1 + t * PART
                    values = piece[:, first : first + PART]
                    for start in starts:
                        past = step + ((2 * block + half) * rows + t * PART * N2 - start)
                        values = jnp.where((past >= 0) & (past < GATE_LEN), 0.0, values)
                    samples[t, at] = values
            return carry

        lax.fori_loop(0, plan.freq, spread, 0)
        for a in range(RADIX_C):
            right = [samples[t, pl.ds(a, PART, stride=RADIX_C)] for t in range(tiles)]
            right = jnp.concatenate([r.astype(jnp.bfloat16) for r in right], axis=1)
            section = lax.dot_general(
                row_table_ref[...],
                right,
                (((1,), (1,)), ((), ())),
                preferred_element_type=jnp.float32,
            )
            re, im = section[:N1], section[N1:]
            tw_re, tw_im = twiddle[a, :, :PART], twiddle[a, :, PART:]
            both = [re * tw_re + im * tw_im, im * tw_re - re * tw_im]
            both = jnp.concatenate(both, axis=1).astype(jnp.bfloat16)
            parts[a] = lax.dot_general(
                both, stage_one[a], (((1,), (1,)), ((), ())), preferred_element_type=jnp.float32
            )

        def finish(block, carry):
            at = pl.ds(pl.multiple_of(block * rows, rows), rows)
            inverse = blocks[block, 1].astype(jnp.float32)
            re = [parts[a, at, :PART] for a in range(RADIX_C)]
            im = [parts[a, at, PART:] for a in range(RADIX_C)]
            for q, (y_im, y_re) in enumerate(dft_eight(im, re)):
                tile = slice(q * PART, (q + 1) * PART)
                out[0, at, tile] = y_re * inverse[:, tile]
                out[1, at, tile] = y_im * inverse[:, tile]
            return carry

        lax.fori_loop(0, plan.freq, finish, 0)


def spectrum_of(plan, rows, where, gates, table_r, stage_one, twiddle, pieces):
    vmem = pl.BlockSpec(memory_space=pltpu.VMEM)
    hbm = pl.BlockSpec(memory_space=pl.ANY)
    return pl.pallas_call(
        functools.partial(spectrum_kernel, plan, rows),
        out_shape=jax.ShapeDtypeStruct((2, N1, N2), jnp.float32),
        in_specs=[*[pl.BlockSpec(memory_space=pltpu.SMEM)] * 2, *[vmem] * 3, *[hbm] * len(pieces)],
        out_specs=vmem,
        scratch_shapes=[
            pltpu.VMEM((plan.freq, 2, rows, N2), jnp.bfloat16),
            pltpu.VMEM((N1 // PART, N2, PART), jnp.float32),
            pltpu.VMEM((RADIX_C, N1, 2 * PART), jnp.float32),
            pltpu.SemaphoreType.DMA,
        ],
        compiler_params=pltpu.CompilerParams(vmem_limit_bytes=40 * 1024 * 1024),
        name="spectrum",
    )(where, gates, table_r, stage_one, twiddle, *pieces)


def total(array):
    return jnp.sum(jnp.sum(array, axis=0, keepdims=True), axis=1, keepdims=True)


def lag_kernel(
    plan, rows, where_ref, spectrum, stage_one, stage_two, twiddle, unscramble, *rest
):
    n_tmpl = plan.planes
    n_piece = 1 + len(plan.bits)
    tmpl_in, rest = rest[:n_tmpl], rest[n_tmpl:]
    small_in, rest = rest[:n_piece], rest[n_piece:]
    own_in, rest = rest[:n_piece], rest[n_piece:]
    other_in, rest = rest[:n_piece], rest[n_piece:]
    outs, rest = rest[: plan.planes], rest[plan.planes :]
    tmpl, psd, basis, prod, weight, inner, score, natural, blocks, acc, sem = rest
    plane, place = where_ref[0], where_ref[1]
    freq, width, planes = plan.freq, plan.width, plan.planes

    @pl.when(plane >= DET)
    def _():
        for ref in outs:
            ref[...] = jnp.zeros_like(ref)

    @pl.when(plane < DET)
    def _():
        def copy_tmpl(ref, source_plane):
            for m in range(width):
                source = source_plane * width + (place ^ plan.offsets[m])
                pltpu.make_async_copy(ref.at[m], tmpl.at[source], sem.at[0]).start()

        for ahead, ref in enumerate(tmpl_in):
            copy_tmpl(ref, lax.rem(plane + ahead, planes))

        from_pieces = functools.partial(from_plane_gather, plan, plane, place)
        from_pieces(
            small_in, lambda src, f: pltpu.make_async_copy(src.at[1], psd.at[f], sem.at[1]).start()
        )
        for j in range(2):
            from_pieces(
                own_in,
                lambda src, f, j=j: pltpu.make_async_copy(
                    src.at[j], basis.at[j, f], sem.at[2]
                ).start(),
            )
            from_pieces(
                other_in,
                lambda src, f, j=j: pltpu.make_async_copy(
                    src.at[j], basis.at[2 + j, f], sem.at[2]
                ).start(),
            )
        pltpu.make_async_copy(tmpl, tmpl, sem.at[0]).wait()
        pltpu.make_async_copy(psd, psd, sem.at[1]).wait()

        def spread_out(block, real, imag):
            tiles = [slice(a * PART, (a + 1) * PART) for a in range(RADIX_C)]
            parts = dft_eight([real[:, t] for t in tiles], [imag[:, t] for t in tiles])
            for c0, (re, im) in enumerate(parts):
                both = jnp.concatenate([re, im], axis=1)
                inner[c0, block] = both.astype(inner.dtype)

        def fold(array):
            return jnp.sum(array.reshape(rows // 8, 8, N2), axis=0)

        acc[...] = jnp.zeros_like(acc)

        def start_block(block, carry):
            at = pl.ds(pl.multiple_of(block * rows, rows), rows)
            t_re = tmpl[block, 0].astype(jnp.float32)
            t_im = tmpl[block, 1].astype(jnp.float32)
            inverse = psd[block].astype(jnp.float32)
            x_re = spectrum[0, at]
            x_im = spectrum[1, at]
            p_re = x_re * t_re + x_im * t_im
            p_im = x_im * t_re - x_re * t_im
            heavy = inverse * inverse * (t_re * t_re + t_im * t_im)
            prod[0, at] = p_re
            prod[1, at] = p_im
            weight[at] = heavy
            acc[0] += fold(heavy)
            spread_out(block, p_re, p_im)
            return carry

        lax.fori_loop(0, freq, start_block, 0)
        variance = total(acc[0])

        def transforms(use):
            def pair(cp, carry):
                columns = [[] for _ in range(RADIX_R)]
                for half in range(2):
                    c0 = 2 * cp + half
                    left = inner[c0].reshape(N1, 2 * PART).astype(jnp.bfloat16)
                    lag = jnp.dot(left, stage_one[c0], preferred_element_type=jnp.float32)
                    g_re, g_im = lag[:, :PART], lag[:, PART:]
                    tw_re, tw_im = twiddle[c0, :, :PART], twiddle[c0, :, PART:]
                    y_re = g_re * tw_re - g_im * tw_im
                    y_im = g_re * tw_im + g_im * tw_re
                    cuts = [slice(a * PART, (a + 1) * PART) for a in range(RADIX_R)]
                    parts = dft_four([y_re[t] for t in cuts], [y_im[t] for t in cuts])
                    for r0, (re, im) in enumerate(parts):
                        columns[r0].append(jnp.concatenate([re, im], axis=0).astype(jnp.bfloat16))
                for r0 in range(RADIX_R):
                    right = jnp.concatenate(columns[r0], axis=1)
                    lag = jnp.dot(stage_two[r0], right, preferred_element_type=jnp.float32)
                    use(cp, r0, lag[:PART], lag[PART:])
                return carry

            lax.fori_loop(0, RADIX_C // 2, pair, 0)

        head_scale = 1.0 / (MODULUS * variance)

        def use_base(cp, r0, re, im):
            score[cp, r0] = (re * re + im * im) * head_scale

        transforms(use_base)
        pltpu.make_async_copy(basis, basis, sem.at[2]).wait()

        acc[...] = jnp.zeros_like(acc)

        def moment_block(block, carry):
            at = pl.ds(pl.multiple_of(block * rows, rows), rows)
            heavy = weight[at]
            for j in range(CAL):
                acc[j] += fold(heavy * basis[j, block].astype(jnp.float32))
            return carry

        lax.fori_loop(0, freq, moment_block, 0)

        def response(j, carry):
            projection = total(acc[j]) / variance
            acc[CAL] = jnp.zeros_like(acc[CAL])

            def filter_block(block, inside):
                at = pl.ds(pl.multiple_of(block * rows, rows), rows)
                centred = basis[j, block].astype(jnp.float32) - projection
                acc[CAL] += fold(weight[at] * centred * centred)
                spread_out(block, prod[0, at] * centred, prod[1, at] * centred)
                return inside

            lax.fori_loop(0, freq, filter_block, 0)
            tail_scale = 1.0 / (MODULUS * total(acc[CAL]))

            def use_tail(cp, r0, re, im):
                score[cp, r0] += (re * re + im * im) * tail_scale

            transforms(use_tail)
            return carry

        lax.fori_loop(0, CAL, response, 0)
        for cp in range(RADIX_C // 2):
            for r0 in range(RADIX_R):
                done = score[cp, r0] * (1.0 / (DET * RESP))
                natural[2 * cp, pl.ds(r0, PART, stride=RADIX_R)] = done[:, :PART]
                natural[2 * cp + 1, pl.ds(r0, PART, stride=RADIX_R)] = done[:, PART:]
        left = jnp.concatenate([natural[c0].astype(jnp.bfloat16) for c0 in range(RADIX_C)], axis=1)
        span = N2 // planes
        whole = jnp.dot(left, unscramble[...], preferred_element_type=jnp.float32)
        for z in range(planes):
            blocks[z] = whole[:, z * span : (z + 1) * span]
        for o, ref in enumerate(outs):
            ref[...] = blocks[lax.rem(plane + o, planes)].astype(jnp.bfloat16)


def lag_scores(plan, rows, where, spectrum, tables, tmpl, small, own, other):
    vmem = pl.BlockSpec(memory_space=pltpu.VMEM)
    hbm = pl.BlockSpec(memory_space=pl.ANY)
    streams = [*tmpl, *small, *own, *other]
    inner_type = jnp.bfloat16 if rows % 16 == 0 else jnp.float32
    return pl.pallas_call(
        functools.partial(lag_kernel, plan, rows),
        out_shape=[jax.ShapeDtypeStruct((N1, N2 // plan.planes), jnp.bfloat16)] * plan.planes,
        in_specs=[pl.BlockSpec(memory_space=pltpu.SMEM), *[vmem] * 5, *[hbm] * len(streams)],
        out_specs=[vmem] * plan.planes,
        scratch_shapes=[
            pltpu.VMEM((plan.freq, 2, rows, N2), jnp.bfloat16),
            pltpu.VMEM((plan.freq, rows, N2), jnp.bfloat16),
            pltpu.VMEM((CAL, plan.freq, rows, N2), jnp.bfloat16),
            pltpu.VMEM((2, N1, N2), jnp.float32),
            pltpu.VMEM((N1, N2), jnp.float32),
            pltpu.VMEM((RADIX_C, plan.freq, rows, 2 * PART), inner_type),
            pltpu.VMEM((RADIX_C // 2, RADIX_R, PART, 2 * PART), jnp.float32),
            pltpu.VMEM((RADIX_C, N1, PART), jnp.float32),
            pltpu.VMEM((plan.planes, N1, N2 // plan.planes), jnp.float32),
            pltpu.VMEM((CAL + 1, 8, N2), jnp.float32),
            pltpu.SemaphoreType.DMA((3,)),
        ],
        compiler_params=pltpu.CompilerParams(vmem_limit_bytes=60 * 1024 * 1024),
        name="lag_scores",
    )(where, spectrum, *tables, *streams)


def on_device(groups, strain, gate_start, psd_inverse, templates, basis):
    freq = lax.axis_size("freq")
    plan = Plan(freq, templates.shape[0], groups)
    me = lax.axis_index("freq")
    group = lax.axis_index("tmpl")
    plane, place = me // plan.width, me % plan.width
    cols, rows = strain.shape[1], psd_inverse.shape[1]

    packed = jnp.concatenate([strain[:, : cols // 2], strain[:, cols // 2 :]], axis=2)
    half = lax.dynamic_slice_in_dim(basis, 2 * (group % 2), 2, 1)
    inverse = psd_inverse.astype(jnp.bfloat16)
    shares = jnp.concatenate([packed[:, None], inverse[:, None], half], axis=1)
    piece = scatter_planes(plan, plane, shares)

    tmpl = scatter_templates(plan, place, templates)
    rings = gather_templates(plan, tmpl)

    small = gather_plane(plan, piece[:, :2])
    other = lax.ppermute(piece[:, 2:], "tmpl", [(g, g ^ 1) for g in range(groups)])
    own = gather_plane(plan, piece[:, 2:])
    other = gather_plane(plan, other)

    where = jnp.stack([plane, place]).astype(jnp.int32)
    zero, _ = lax.optimization_barrier((jnp.int32(0), tmpl))
    stage_one, twiddle = column_tables(zero)
    table_r = row_table(zero)
    stage_two, unscramble = lag_tables(zero)
    spectrum = spectrum_of(plan, rows, where, gate_start, table_r, stage_one, twiddle, small)
    scores = lag_scores(
        plan,
        rows,
        where,
        spectrum,
        (stage_one, stage_two, twiddle, unscramble),
        rings,
        small,
        own,
        other,
    )

    summed = scores[0].astype(jnp.float32)
    for o in range(1, plan.planes):
        got = lax.ppermute(scores[o], "freq", plan.shift_out(o))
        summed = summed + got.astype(jnp.float32)
    best = summed.astype(jnp.bfloat16)
    for b in plan.bits:
        side = (place // b) % 2
        span = best.shape[1] // 2
        send = lax.dynamic_slice_in_dim(best, (1 - side) * span, span, 1)
        keep = lax.dynamic_slice_in_dim(best, side * span, span, 1)
        best = jnp.maximum(keep, lax.ppermute(send, "freq", plan.swap(b)))
    b = groups // 2
    while b:
        side = (group // b) % 2
        span = best.shape[0] // 2
        send = lax.dynamic_slice_in_dim(best, (1 - side) * span, span, 0)
        keep = lax.dynamic_slice_in_dim(best, side * span, span, 0)
        swap = [(g, g ^ b) for g in range(groups)]
        best = jnp.maximum(keep, lax.ppermute(send, "tmpl", swap))
        b //= 2
    return best.astype(jnp.float32)


def solution(mesh):
    def whole(*args):
        return on_device(mesh.shape["tmpl"], *args)

    placed = (
        P(None, "freq", None),
        P(),
        P(None, "freq", None),
        P("tmpl", None, "freq", None),
        P(None, None, "freq", None),
    )
    return jax.shard_map(
        whole, mesh=mesh, in_specs=placed, out_specs=P("tmpl", "freq"), check_vma=False
    )
```

profile of v0, /device:TPU:26, one launch (start us, length us, event | category | flops | bytes accessed | tf_op | source)
XLA Modules:
  0.0 162.0 jit_solution(6975363175507510532)
XLA Ops:
  2.4 2.1 %collective-permute-start.2 = (bf16[4,32,1024]{2,1,0:T(8,128)(2,1)S(1)}, bf16[4,32,1024]{2,1,0:T(8,128)(2,1)S(1)}, u32[]{:S(2)}, u32[]{:S(2)}) collective-permute-start(bf16[4,32,1024]{2,1,0:T(8,128)(2,1)S(1)} %get-tuple-element.21), channel_id=1, source_target_pairs={{0,4},{1,5},{2,6},{3,7},{4,8},{5,9},{6,10},{7,11},{12,0},{13,1},{1... | collective-permute-start | bytes 786440 | tf_op jit(solution)/shard_map/ppermute | solution.py:118
  4.5 4.3 %collective-permute-start.3 = (bf16[4,32,1024]{2,1,0:T(8,128)(2,1)S(1)}, bf16[4,32,1024]{2,1,0:T(8,128)(2,1)}, u32[]{:S(2)}, u32[]{:S(2)}) collective-permute-start(bf16[4,32,1024]{2,1,0:T(8,128)(2,1)S(1)} %get-tuple-element.20), channel_id=1, source_target_pairs={{0,8},{1,9},{2,10},{3,11},{8,0},{9,1},{10,2},{11,3},{12,4},{13,5},... | collective-permute-start | bytes 786440 | tf_op jit(solution)/shard_map/ppermute | solution.py:118
  8.8 2.4 %collective-permute-start.4 = (bf16[4,32,1024]{2,1,0:T(8,128)(2,1)S(1)}, bf16[4,32,1024]{2,1,0:T(8,128)(2,1)}, u32[]{:S(2)}, u32[]{:S(2)}) collective-permute-start(bf16[4,32,1024]{2,1,0:T(8,128)(2,1)S(1)} %get-tuple-element.19), channel_id=1, source_target_pairs={{4,0},{5,1},{6,2},{7,3},{8,4},{9,5},{10,6},{11,7},{12,8},{13,9},{1... | collective-permute-start | bytes 786440 | tf_op jit(solution)/shard_map/ppermute | solution.py:118
  12.0 6.5 %collective-permute-done = bf16[1,2,2,32,1024]{4,3,2,0,1:T(8,128)(2,1)S(1)} collective-permute-done((bf16[1,2,2,32,1024]{4,3,2,0,1:T(8,128)(2,1)S(1)}, bf16[1,2,2,32,1024]{4,3,2,0,1:T(8,128)(2,1)S(1)}, u32[]{:S(2)}, u32[]{:S(2)}) %collective-permute-start) | collective-permute-done | bytes 262176 | tf_op jit(solution)/shard_map/ppermute | solution.py:137
  18.6 2.7 %collective-permute-done.4 = bf16[4,32,1024]{2,1,0:T(8,128)(2,1)} collective-permute-done((bf16[4,32,1024]{2,1,0:T(8,128)(2,1)S(1)}, bf16[4,32,1024]{2,1,0:T(8,128)(2,1)}, u32[]{:S(2)}, u32[]{:S(2)}) %collective-permute-start.4) | collective-permute-done | bytes 262176 | tf_op jit(solution)/shard_map/ppermute | solution.py:118
  22.7 1.6 collective-permute-start.12
  24.8 1.5 collective-permute-start.5
  26.4 7.1 %collective-permute-start.7 = (bf16[4,2,32,1024]{3,2,1,0:T(8,128)(2,1)S(1)}, bf16[4,2,32,1024]{3,2,1,0:T(8,128)(2,1)S(1)}, u32[]{:S(2)}, u32[]{:S(2)}) collective-permute-start(bf16[4,2,32,1024]{3,2,1,0:T(8,128)(2,1)S(1)} %maximum_bitcast_fusion.rest_0_), channel_id=1, source_target_pairs={{0,12},{1,13},{2,14},{3,15},{4,0},{5,1},{6,2},{7,3},{8,4},{9,5},{1... | collective-permute-start | bytes 1572872 | tf_op jit(solution)/shard_map/ppermute | solution.py:145
  37.3 2.2 %fusion.15 = (bf16[8,128,128]{2,1,0:T(8,128)(2,1)S(1)}, bf16[8,128,128]{2,1,0:T(8,128)(2,1)S(1)}, bf16[8,128,128]{2,1,0:T(8,128)(2,1)S(1)}) fusion(s32[8,128]{1,0:T(8,128)S(1)} %get-tuple-element.47), kind=kLoop, calls=%fused_computation.49 | loop fusion | flops 2359296 | bytes 790528 | tf_op jit(solution)/shard_map/convert.11
  39.8 10.5 %collective-permute-done.5.rest_1_.rest_5_ = bf16[1,4,2,32,1024]{4,3,2,1,0:T(8,128)(2,1)S(1)} collective-permute-done((bf16[1,4,2,32,1024]{4,3,2,1,0:T(8,128)(2,1)S(1)}, bf16[1,4,2,32,1024]{4,3,2,1,0:T(8,128)(2,1)S(1)}, u32[]{:S(2)}, u32[]{:S(2)}) %collective-permute-start.5) | collective-permute-done | bytes 524320 | tf_op jit(solution)/shard_map/ppermute | solution.py:126
  50.5 7.1 %collective-permute-start.8 = (bf16[4,2,32,1024]{3,2,1,0:T(8,128)(2,1)S(1)}, bf16[4,2,32,1024]{3,2,1,0:T(8,128)(2,1)S(1)}, u32[]{:S(2)}, u32[]{:S(2)}) collective-permute-start(bf16[4,2,32,1024]{3,2,1,0:T(8,128)(2,1)S(1)} %collective-permute-done.7.rest_1_), channel_id=1, source_target_pairs={{0,12},{1,13},{2,14},{3,15},{4,0},{5,1},{6,2},{7,3},{8,4},{9,5},{1... | collective-permute-start | bytes 1572872 | tf_op jit(solution)/shard_map/ppermute | solution.py:145
  57.6 1.7 %collective-permute-done.13.rest_11_ = bf16[1,4,2,32,1024]{4,3,2,1,0:T(8,128)(2,1)S(1)} collective-permute-done((bf16[1,4,2,32,1024]{4,3,2,1,0:T(8,128)(2,1)S(1)}, bf16[1,4,2,32,1024]{4,3,2,1,0:T(8,128)(2,1)S(1)}, u32[]{:S(2)}, u32[]{:S(2)}) %collective-permute-start.13) | collective-permute-done | bytes 524320 | tf_op jit(solution)/shard_map/ppermute | solution.py:126
  60.2 9.1 %collective-permute-done.8.rest_2_ = bf16[4,2,32,1024]{3,2,1,0:T(8,128)(2,1)S(1)} collective-permute-done((bf16[4,2,32,1024]{3,2,1,0:T(8,128)(2,1)S(1)}, bf16[4,2,32,1024]{3,2,1,0:T(8,128)(2,1)S(1)}, u32[]{:S(2)}, u32[]{:S(2)}) %collective-permute-start.8) | collective-permute-done | bytes 524320 | tf_op jit(solution)/shard_map/ppermute | solution.py:145
  69.4 2.6 %collective-permute-start.9 = (bf16[4,2,32,1024]{3,2,1,0:T(8,128)(2,1)S(1)}, bf16[4,2,32,1024]{3,2,1,0:T(8,128)(2,1)S(1)}, u32[]{:S(2)}, u32[]{:S(2)}) collective-permute-start(bf16[4,2,32,1024]{3,2,1,0:T(8,128)(2,1)S(1)} %collective-permute-done.8.rest_2_), channel_id=1, source_target_pairs={{0,12},{1,13},{2,14},{3,15},{4,0},{5,1},{6,2},{7,3},{8,4},{9,5},{1... | collective-permute-start | bytes 1572872 | tf_op jit(solution)/shard_map/ppermute | solution.py:145
  73.1 2.0 %fusion.unscramble = bf16[1024,1024]{1,0:T(8,128)(2,1)} fusion(s32[1024]{0:T(1024)S(1)} %get-tuple-element.46), kind=kLoop, calls=%fused_computation.2 | loop fusion | flops 2097152 | bytes 2101248 | tf_op jit(solution)/shard_map/convert_element_type | solution.py:77
  76.2 2.0 %copy-done.2 = f32[2,512,1024]{2,1,0:T(8,128)} copy-done((f32[2,512,1024]{2,1,0:T(8,128)}, f32[2,512,1024]{2,1,0:T(8,128)S(1)}, u32[]{:S(2)}) %copy-start.2) | copy-done | bytes 4194328
  79.2 6.3 %collective-permute-done.9.rest_3_ = bf16[4,2,32,1024]{3,2,1,0:T(8,128)(2,1)S(1)} collective-permute-done((bf16[4,2,32,1024]{3,2,1,0:T(8,128)(2,1)S(1)}, bf16[4,2,32,1024]{3,2,1,0:T(8,128)(2,1)S(1)}, u32[]{:S(2)}, u32[]{:S(2)}) %collective-permute-start.9) | collective-permute-done | bytes 524320 | tf_op jit(solution)/shard_map/ppermute | solution.py:145
  86.3 5.8 %lag_scores.1 = (bf16[512,256]{1,0:T(8,128)(2,1)}, bf16[512,256]{1,0:T(8,128)(2,1)}, bf16[512,256]{1,0:T(8,128)(2,1)}, bf16[512,256]{1,0:T(8,128)(2,1)}) custom-call(s32[2]{0:T(128)} %copy-done.7, f32[2,512,1024]{2,1,0:T(8,128)} %copy-done.2, bf16[8,256,256]{2,1,0:T(8,128)(2,1)} %copy-done.3, bf16[4,256,256]{2,1,0:T(8,128)(2,1)} %maximum_maximum_fusion.1.stage_two, ...), custom_call_target="tpu_custom_call" | custom-call | tf_op jit(solution)/shard_map/lag_scores/pallas_call | solution.py:456
  92.1 1.3 collective-permute-start.15
  96.0 35.3 %collective-permute-done.15 = bf16[512,256]{1,0:T(8,128)(2,1)S(1)} collective-permute-done((bf16[512,256]{1,0:T(8,128)(2,1)}, bf16[512,256]{1,0:T(8,128)(2,1)S(1)}, u32[]{:S(2)}, u32[]{:S(2)}) %collective-permute-start.15) | collective-permute-done | bytes 262176 | tf_op jit(solution)/shard_map/ppermute | solution.py:521
  131.3 17.8 %collective-permute-done.16 = bf16[512,256]{1,0:T(8,128)(2,1)S(1)} collective-permute-done((bf16[512,256]{1,0:T(8,128)(2,1)}, bf16[512,256]{1,0:T(8,128)(2,1)S(1)}, u32[]{:S(2)}, u32[]{:S(2)}) %collective-permute-start.16) | collective-permute-done | bytes 262176 | tf_op jit(solution)/shard_map/ppermute | solution.py:521
  150.8 4.4 %collective-permute-done.18 = bf16[512,128]{1,0:T(8,128)(2,1)S(1)} collective-permute-done((bf16[512,128]{1,0:T(8,128)(2,1)S(1)}, bf16[512,128]{1,0:T(8,128)(2,1)S(1)}, u32[]{:S(2)}, u32[]{:S(2)}) %collective-permute-start.18) | collective-permute-done | bytes 131104 | tf_op jit(solution)/shard_map/ppermute | solution.py:529
  155.5 1.3 collective-permute-done.19
  157.5 3.8 %collective-permute-done.20 = bf16[256,64]{1,0:T(8,128)(2,1)S(1)} collective-permute-done((bf16[256,64]{1,0:T(8,128)(2,1)S(1)}, bf16[256,64]{1,0:T(8,128)(2,1)S(1)}, u32[]{:S(2)}, u32[]{:S(2)}) %collective-permute-start.20) | collective-permute-done | bytes 32800 | tf_op jit(solution)/shard_map/ppermute | solution.py:537
  (103 shorter events, 20.1 us)
Async XLA Ops:
  2.4 16.3 %collective-permute-start.2 = (bf16[4,32,1024]{2,1,0:T(8,128)(2,1)S(1)}, bf16[4,32,1024]{2,1,0:T(8,128)(2,1)S(1)}, u32[]{:S(2)}, u32[]{:S(2)}) collective-permute-start(bf16[4,32,1024]{2,1,0:T(8,128)(2,1)S(1)} %get-tuple-element.21), channel_id=1, source_target_pairs={{0,4},{1,5},{2,6},{3,7},{4,8},{5,9},{6,10},{7,11},{12,0},{13,1},{1... | collective-permute-start | bytes 786440 | tf_op jit(solution)/shard_map/ppermute | solution.py:118
  4.5 14.1 %collective-permute-start.3 = (bf16[4,32,1024]{2,1,0:T(8,128)(2,1)S(1)}, bf16[4,32,1024]{2,1,0:T(8,128)(2,1)}, u32[]{:S(2)}, u32[]{:S(2)}) collective-permute-start(bf16[4,32,1024]{2,1,0:T(8,128)(2,1)S(1)} %get-tuple-element.20), channel_id=1, source_target_pairs={{0,8},{1,9},{2,10},{3,11},{8,0},{9,1},{10,2},{11,3},{12,4},{13,5},... | collective-permute-start | bytes 786440 | tf_op jit(solution)/shard_map/ppermute | solution.py:118
  8.8 12.5 %collective-permute-start.4 = (bf16[4,32,1024]{2,1,0:T(8,128)(2,1)S(1)}, bf16[4,32,1024]{2,1,0:T(8,128)(2,1)}, u32[]{:S(2)}, u32[]{:S(2)}) collective-permute-start(bf16[4,32,1024]{2,1,0:T(8,128)(2,1)S(1)} %get-tuple-element.19), channel_id=1, source_target_pairs={{4,0},{5,1},{6,2},{7,3},{8,4},{9,5},{10,6},{11,7},{12,8},{13,9},{1... | collective-permute-start | bytes 786440 | tf_op jit(solution)/shard_map/ppermute | solution.py:118
  11.2 7.3 %collective-permute-start = (bf16[1,2,2,32,1024]{4,3,2,0,1:T(8,128)(2,1)S(1)}, bf16[1,2,2,32,1024]{4,3,2,0,1:T(8,128)(2,1)S(1)}, u32[]{:S(2)}, u32[]{:S(2)}) collective-permute-start(bf16[1,2,2,32,1024]{4,3,2,0,1:T(8,128)(2,1)S(1)} %get-tuple-element.24), channel_id=1, source_target_pairs={{0,2},{1,3},{2,0},{3,1},{4,6},{5,7},{6,4},{7,5},{8,10},{9,11},{10,... | collective-permute-start | bytes 786440 | tf_op jit(solution)/shard_map/ppermute | solution.py:137
  12.0 63.2 %copy-start.7 = (s32[2]{0:T(128)}, s32[2]{0:T(128)S(1)}, u32[]{:S(2)}) copy-start(s32[2]{0:T(128)S(1)} %pad_add_fusion.where_ref) | copy-start | bytes 28
  18.5 7.7 %collective-permute-start.1 = (bf16[2,1,2,32,1024]{4,3,2,0,1:T(8,128)(2,1)S(1)}, bf16[2,1,2,32,1024]{4,3,2,0,1:T(8,128)(2,1)S(1)}, u32[]{:S(2)}, u32[]{:S(2)}) collective-permute-start(bf16[2,1,2,32,1024]{4,3,2,0,1:T(8,128)(2,1)S(1)} %get-tuple-element.23), channel_id=1, source_target_pairs={{0,1},{1,0},{2,3},{3,2},{4,5},{5,4},{6,7},{7,6},{8,9},{9,8},{10,11... | collective-permute-start | bytes 786440 | tf_op jit(solution)/shard_map/ppermute | solution.py:137
  22.7 52.5 %copy-start.4 = (bf16[1,4,2,32,1024]{4,3,2,1,0:T(8,128)(2,1)}, bf16[1,4,2,32,1024]{4,3,2,1,0:T(8,128)(2,1)S(1)}, u32[]{:S(2)}) copy-start(bf16[1,4,2,32,1024]{4,3,2,1,0:T(8,128)(2,1)S(1)} %get-tuple-element.17.rest_0_.rest_4_) | copy-start | bytes 1572868
  22.7 14.0 %collective-permute-start.12 = (bf16[4,2,32,1024]{3,2,1,0:T(8,128)(2,1)S(1)}, bf16[4,2,32,1024]{3,2,1,0:T(8,128)(2,1)S(1)}, u32[]{:S(2)}, u32[]{:S(2)}) collective-permute-start(bf16[4,2,32,1024]{3,2,1,0:T(8,128)(2,1)S(1)} %get-tuple-element.15), channel_id=1, source_target_pairs={{0,16},{16,0},{1,17},{17,1},{2,18},{18,2},{3,19},{19,3},{4,20},{20... | collective-permute-start | bytes 1572872 | tf_op jit(solution)/shard_map/ppermute | solution.py:497
  24.3 15.3 %collective-permute-start.10 = (bf16[1,4,2,32,1024]{4,3,2,1,0:T(8,128)(2,1)S(1)}, bf16[1,4,2,32,1024]{4,3,2,1,0:T(8,128)(2,1)S(1)}, u32[]{:S(2)}, u32[]{:S(2)}) collective-permute-start(bf16[1,4,2,32,1024]{4,3,2,1,0:T(8,128)(2,1)S(1)} %get-tuple-element.16.rest_7_), channel_id=1, source_target_pairs={{0,2},{1,3},{2,0},{3,1},{4,6},{5,7},{6,4},{7,5},{8,10},{9,11},{10,... | collective-permute-start | bytes 1572872 | tf_op jit(solution)/shard_map/ppermute | solution.py:126
  24.8 25.5 %collective-permute-start.5 = (bf16[1,4,2,32,1024]{4,3,2,1,0:T(8,128)(2,1)S(1)}, bf16[1,4,2,32,1024]{4,3,2,1,0:T(8,128)(2,1)S(1)}, u32[]{:S(2)}, u32[]{:S(2)}) collective-permute-start(bf16[1,4,2,32,1024]{4,3,2,1,0:T(8,128)(2,1)S(1)} %get-tuple-element.17.rest_0_.rest_4_), channel_id=1, source_target_pairs={{0,2},{1,3},{2,0},{3,1},{4,6},{5,7},{6,4},{7,5},{8,10},{9,11},{10,... | collective-permute-start | bytes 1572872 | tf_op jit(solution)/shard_map/ppermute | solution.py:126
  26.4 24.1 %collective-permute-start.7 = (bf16[4,2,32,1024]{3,2,1,0:T(8,128)(2,1)S(1)}, bf16[4,2,32,1024]{3,2,1,0:T(8,128)(2,1)S(1)}, u32[]{:S(2)}, u32[]{:S(2)}) collective-permute-start(bf16[4,2,32,1024]{3,2,1,0:T(8,128)(2,1)S(1)} %maximum_bitcast_fusion.rest_0_), channel_id=1, source_target_pairs={{0,12},{1,13},{2,14},{3,15},{4,0},{5,1},{6,2},{7,3},{8,4},{9,5},{1... | collective-permute-start | bytes 1572872 | tf_op jit(solution)/shard_map/ppermute | solution.py:145
  36.7 22.6 %collective-permute-start.13 = (bf16[1,4,2,32,1024]{4,3,2,1,0:T(8,128)(2,1)S(1)}, bf16[1,4,2,32,1024]{4,3,2,1,0:T(8,128)(2,1)S(1)}, u32[]{:S(2)}, u32[]{:S(2)}) collective-permute-start(bf16[1,4,2,32,1024]{4,3,2,1,0:T(8,128)(2,1)S(1)} %bitcast.35), channel_id=1, source_target_pairs={{0,2},{1,3},{2,0},{3,1},{4,6},{5,7},{6,4},{7,5},{8,10},{9,11},{10,... | collective-permute-start | bytes 1572872 | tf_op jit(solution)/shard_map/ppermute | solution.py:126
  39.7 38.5 %collective-permute-start.11 = (bf16[2,4,2,32,1024]{4,3,2,1,0:T(8,128)(2,1)S(1)}, bf16[2,4,2,32,1024]{4,3,2,1,0:T(8,128)(2,1)S(1)}, u32[]{:S(2)}, u32[]{:S(2)}) collective-permute-start(bf16[2,4,2,32,1024]{4,3,2,1,0:T(8,128)(2,1)S(1)} %pad_maximum_fusion.4), channel_id=1, source_target_pairs={{0,1},{1,0},{2,3},{3,2},{4,5},{5,4},{6,7},{7,6},{8,9},{9,8},{10,11... | collective-permute-start | bytes 3145736 | tf_op jit(solution)/shard_map/ppermute | solution.py:126
  50.3 24.9 %copy-start.5 = (bf16[1,4,2,32,1024]{4,3,2,1,0:T(8,128)(2,1)}, bf16[1,4,2,32,1024]{4,3,2,1,0:T(8,128)(2,1)S(1)}, u32[]{:S(2)}) copy-start(bf16[1,4,2,32,1024]{4,3,2,1,0:T(8,128)(2,1)S(1)} %collective-permute-done.5.rest_1_.rest_5_) | copy-start | bytes 1572868
  50.4 24.8 %collective-permute-start.6 = (bf16[2,4,2,32,1024]{4,3,2,1,0:T(8,128)(2,1)S(1)}, bf16[2,4,2,32,1024]{4,3,2,1,0:T(8,128)(2,1)S(1)}, u32[]{:S(2)}, u32[]{:S(2)}) collective-permute-start(bf16[2,4,2,32,1024]{4,3,2,1,0:T(8,128)(2,1)S(1)} %pad_maximum_fusion.3), channel_id=1, source_target_pairs={{0,1},{1,0},{2,3},{3,2},{4,5},{5,4},{6,7},{7,6},{8,9},{9,8},{10,11... | collective-permute-start | bytes 3145736 | tf_op jit(solution)/shard_map/ppermute | solution.py:126
  50.5 18.9 %collective-permute-start.8 = (bf16[4,2,32,1024]{3,2,1,0:T(8,128)(2,1)S(1)}, bf16[4,2,32,1024]{3,2,1,0:T(8,128)(2,1)S(1)}, u32[]{:S(2)}, u32[]{:S(2)}) collective-permute-start(bf16[4,2,32,1024]{3,2,1,0:T(8,128)(2,1)S(1)} %collective-permute-done.7.rest_1_), channel_id=1, source_target_pairs={{0,12},{1,13},{2,14},{3,15},{4,0},{5,1},{6,2},{7,3},{8,4},{9,5},{1... | collective-permute-start | bytes 1572872 | tf_op jit(solution)/shard_map/ppermute | solution.py:145
  59.4 27.0 %collective-permute-start.14 = (bf16[2,4,2,32,1024]{4,3,2,1,0:T(8,128)(2,1)S(1)}, bf16[2,4,2,32,1024]{4,3,2,1,0:T(8,128)(2,1)}, u32[]{:S(2)}, u32[]{:S(2)}) collective-permute-start(bf16[2,4,2,32,1024]{4,3,2,1,0:T(8,128)(2,1)S(1)} %pad_maximum_fusion.5), channel_id=1, source_target_pairs={{0,1},{1,0},{2,3},{3,2},{4,5},{5,4},{6,7},{7,6},{8,9},{9,8},{10,11... | collective-permute-start | bytes 3145736 | tf_op jit(solution)/shard_map/ppermute | solution.py:126
  69.4 16.2 %collective-permute-start.9 = (bf16[4,2,32,1024]{3,2,1,0:T(8,128)(2,1)S(1)}, bf16[4,2,32,1024]{3,2,1,0:T(8,128)(2,1)S(1)}, u32[]{:S(2)}, u32[]{:S(2)}) collective-permute-start(bf16[4,2,32,1024]{3,2,1,0:T(8,128)(2,1)S(1)} %collective-permute-done.8.rest_2_), channel_id=1, source_target_pairs={{0,12},{1,13},{2,14},{3,15},{4,0},{5,1},{6,2},{7,3},{8,4},{9,5},{1... | collective-permute-start | bytes 1572872 | tf_op jit(solution)/shard_map/ppermute | solution.py:145
  92.1 39.2 %collective-permute-start.15 = (bf16[512,256]{1,0:T(8,128)(2,1)}, bf16[512,256]{1,0:T(8,128)(2,1)S(1)}, u32[]{:S(2)}, u32[]{:S(2)}) collective-permute-start(bf16[512,256]{1,0:T(8,128)(2,1)} %get-tuple-element.12), channel_id=1, source_target_pairs={{0,4},{1,5},{2,6},{3,7},{4,8},{5,9},{6,10},{7,11},{8,12},{9,13},{1... | collective-permute-start | bytes 786440 | tf_op jit(solution)/shard_map/ppermute | solution.py:521
  93.4 55.7 %collective-permute-start.16 = (bf16[512,256]{1,0:T(8,128)(2,1)}, bf16[512,256]{1,0:T(8,128)(2,1)S(1)}, u32[]{:S(2)}, u32[]{:S(2)}) collective-permute-start(bf16[512,256]{1,0:T(8,128)(2,1)} %get-tuple-element.13), channel_id=1, source_target_pairs={{0,8},{1,9},{2,10},{3,11},{4,12},{5,13},{6,14},{7,15},{8,0},{9,1},... | collective-permute-start | bytes 786440 | tf_op jit(solution)/shard_map/ppermute | solution.py:521
  94.7 54.4 %collective-permute-start.17 = (bf16[512,256]{1,0:T(8,128)(2,1)}, bf16[512,256]{1,0:T(8,128)(2,1)S(1)}, u32[]{:S(2)}, u32[]{:S(2)}) collective-permute-start(bf16[512,256]{1,0:T(8,128)(2,1)} %get-tuple-element.14), channel_id=1, source_target_pairs={{0,12},{1,13},{2,14},{3,15},{4,0},{5,1},{6,2},{7,3},{8,4},{9,5},{1... | collective-permute-start | bytes 786440 | tf_op jit(solution)/shard_map/ppermute | solution.py:521
  150.2 5.0 %collective-permute-start.18 = (bf16[512,128]{1,0:T(8,128)(2,1)S(1)}, bf16[512,128]{1,0:T(8,128)(2,1)S(1)}, u32[]{:S(2)}, u32[]{:S(2)}) collective-permute-start(bf16[512,128]{1,0:T(8,128)(2,1)S(1)} %constant_dynamic-slice_fusion.2), channel_id=1, source_target_pairs={{0,2},{1,3},{2,0},{3,1},{4,6},{5,7},{6,4},{7,5},{8,10},{9,11},{10,... | collective-permute-start | bytes 393224 | tf_op jit(solution)/shard_map/ppermute | solution.py:529
  155.4 1.4 collective-permute-start.19
  157.0 4.3 %collective-permute-start.20 = (bf16[256,64]{1,0:T(8,128)(2,1)S(1)}, bf16[256,64]{1,0:T(8,128)(2,1)S(1)}, u32[]{:S(2)}, u32[]{:S(2)}) collective-permute-start(bf16[256,64]{1,0:T(8,128)(2,1)S(1)} %constant_dynamic-slice_fusion), channel_id=1, source_target_pairs={{0,16},{16,0},{1,17},{17,1},{2,18},{18,2},{3,19},{19,3},{4,20},{20... | collective-permute-start | bytes 98312 | tf_op jit(solution)/shard_map/ppermute | solution.py:537
  (16 other events, 119.6 us)
where the time goes:
time: 162 us
  waiting for transfers between devices  99.4 us (61%)
  starting transfers between devices  35.8 us (22%)
  other arithmetic  13.4 us (8%)
  local copies, waits for them, and re-layouts  6.54 us (4%)
  Pallas kernels  6.38 us (4%)
    ppermute x3, waiting for transfers between devices, on_device(): got = lax.ppermute(scores[o], 'freq', plan.shift_out(o))  53.1 us
    ppermute x3, starting transfers between devices, gather_templates(): pieces.append(lax.ppermute(pieces[-1], 'freq', plan.back()))  16.8 us
    ppermute x3, waiting for transfers between devices, gather_templates(): pieces.append(lax.ppermute(pieces[-1], 'freq', plan.back()))  15.4 us
    ppermute x6, waiting for transfers between devices, gather_plane(): got = lax.ppermute(held, 'freq', plan.swap(b))  12.2 us
    ppermute x3, starting transfers between devices, scatter_planes(): got.append(lax.ppermute(send, 'freq', plan.shift_in(o)))  8.8 us
    ppermute x2, waiting for transfers between devices, scatter_templates(): got = lax.ppermute(pick(halves, 1 - mine, 1), 'freq', plan.swap(b))  6.49 us
    pallas_call x1, Pallas kernels, lag_scores(): pl.pallas_call(functools.partial(lag_kernel, plan, rows), out_shape=[jax....  5.79 us
    ppermute x2, waiting for transfers between devices, on_device(): best = jnp.maximum(keep, lax.ppermute(send, 'freq', plan.swap(b)))  5.76 us
  transfers between devices with their start and end apart: 21, of which 11 were waited for; matrix products, arithmetic and copies ran while one was open for 7% of the time, Pallas kernels for 0%

commit v1 on v0

--- a/solution.py
+++ b/solution.py
@@ -65,17 +65,13 @@
     coarse = 32 * iota(N1 // 32)
     high = phase(coarse[None, :, None] * cols[:, None, :], MODULUS)
     low = phase(iota(32)[None, :, None] * cols[:, None, :], MODULUS)
-    real, imag = times([h[:, :, None] for h in high], [w[:, None] for w in low])
-    twiddle = jnp.concatenate([real, imag], axis=3).reshape(RADIX_C, N1, 2 * PART)
-    return stage_one, twiddle
+    return stage_one, jnp.stack(high), jnp.stack(low)
 
 
 def lag_tables(zero):
     rows = zero + iota(RADIX_R)[:, None] + RADIX_R * iota(PART)[None, :]
     stage_two = block_table(*phase(rows[:, :, None] * iota(PART)[None, None, :], N1), True)
-    order = lag_columns(zero).reshape(-1)
-    unscramble = (order[:, None] == iota(N2)[None, :]).astype(jnp.bfloat16)
-    return stage_two, unscramble
+    return stage_two
 
 
 class Plan:
@@ -201,9 +197,11 @@
             m += 1
 
 
-def spectrum_kernel(plan, rows, where_ref, gates_ref, row_table_ref, stage_one, twiddle, *rest):
+def spectrum_kernel(
+    plan, rows, where_ref, gates_ref, row_table_ref, stage_one, coarse_ref, fine_ref, *rest
+):
     pieces, rest = rest[: 1 + len(plan.bits)], rest[1 + len(plan.bits) :]
-    out, blocks, samples, parts, sem = rest
+    out, twiddle, unscramble, blocks, samples, parts, sem = rest
     plane, place = where_ref[0], where_ref[1]
 
     @pl.when(plane < DET)
@@ -215,6 +213,23 @@
             pieces,
             lambda src, f: pltpu.make_async_copy(src, blocks.at[f], sem).start(),
         )
+
+        def twiddle_of(c0, carry):
+            fine_re, fine_im = fine_ref[0, c0], fine_ref[1, c0]
+            span = fine_re.shape[0]
+            for a in range(N1 // span):
+                high = coarse_ref[0, c0, a : a + 1], coarse_ref[1, c0, a : a + 1]
+                re, im = times(high, (fine_re, fine_im))
+                twiddle[c0, a * span : (a + 1) * span, :PART] = re
+                twiddle[c0, a * span : (a + 1) * span, PART:] = im
+            return carry
+
+        lax.fori_loop(0, RADIX_C, twiddle_of, 0)
+        row = lax.broadcasted_iota(jnp.int32, (PART, N2), 0)
+        column = lax.broadcasted_iota(jnp.int32, (PART, N2), 1)
+        for c0 in range(RADIX_C):
+            hit = column == c0 + RADIX_C * row
+            unscramble[c0 * PART : (c0 + 1) * PART] = jnp.where(hit, 1.0, 0.0).astype(jnp.bfloat16)
         pltpu.make_async_copy(blocks, blocks, sem).wait()
         tiles = N1 // PART
 
@@ -236,22 +251,26 @@
             return carry
 
         lax.fori_loop(0, plan.freq, spread, 0)
-        for a in range(RADIX_C):
-            right = [samples[t, pl.ds(a, PART, stride=RADIX_C)] for t in range(tiles)]
-            right = jnp.concatenate([r.astype(jnp.bfloat16) for r in right], axis=1)
+        for first in range(0, RADIX_C, 2):
+            right = []
+            for a in (first, first + 1):
+                found = [samples[t, pl.ds(a, PART, stride=RADIX_C)] for t in range(tiles)]
+                right.append(jnp.concatenate([r.astype(jnp.bfloat16) for r in found], axis=1))
             section = lax.dot_general(
                 row_table_ref[...],
-                right,
+                jnp.concatenate(right, axis=0),
                 (((1,), (1,)), ((), ())),
                 preferred_element_type=jnp.float32,
             )
-            re, im = section[:N1], section[N1:]
-            tw_re, tw_im = twiddle[a, :, :PART], twiddle[a, :, PART:]
-            both = [re * tw_re + im * tw_im, im * tw_re - re * tw_im]
-            both = jnp.concatenate(both, axis=1).astype(jnp.bfloat16)
-            parts[a] = lax.dot_general(
-                both, stage_one[a], (((1,), (1,)), ((), ())), preferred_element_type=jnp.float32
-            )
+            for a in (first, first + 1):
+                lanes = slice((a - first) * PART, (a - first + 1) * PART)
+                re, im = section[:N1, lanes], section[N1:, lanes]
+                tw_re, tw_im = twiddle[a, :, :PART], twiddle[a, :, PART:]
+                both = [re * tw_re + im * tw_im, im * tw_re - re * tw_im]
+                both = jnp.concatenate(both, axis=1).astype(jnp.bfloat16)
+                parts[a] = lax.dot_general(
+                    both, stage_one[a], (((1,), (1,)), ((), ())), preferred_element_type=jnp.float32
+                )
 
         def finish(block, carry):
             at = pl.ds(pl.multiple_of(block * rows, rows), rows)
@@ -267,14 +286,18 @@
         lax.fori_loop(0, plan.freq, finish, 0)
 
 
-def spectrum_of(plan, rows, where, gates, table_r, stage_one, twiddle, pieces):
+def spectrum_of(plan, rows, where, gates, table_r, stage_one, coarse, fine, pieces):
     vmem = pl.BlockSpec(memory_space=pltpu.VMEM)
     hbm = pl.BlockSpec(memory_space=pl.ANY)
     return pl.pallas_call(
         functools.partial(spectrum_kernel, plan, rows),
-        out_shape=jax.ShapeDtypeStruct((2, N1, N2), jnp.float32),
-        in_specs=[*[pl.BlockSpec(memory_space=pltpu.SMEM)] * 2, *[vmem] * 3, *[hbm] * len(pieces)],
-        out_specs=vmem,
+        out_shape=[
+            jax.ShapeDtypeStruct((2, N1, N2), jnp.float32),
+            jax.ShapeDtypeStruct((RADIX_C, N1, 2 * PART), jnp.float32),
+            jax.ShapeDtypeStruct((N2, N2), jnp.bfloat16),
+        ],
+        in_specs=[*[pl.BlockSpec(memory_space=pltpu.SMEM)] * 2, *[vmem] * 4, *[hbm] * len(pieces)],
+        out_specs=[vmem] * 3,
         scratch_shapes=[
             pltpu.VMEM((plan.freq, 2, rows, N2), jnp.bfloat16),
             pltpu.VMEM((N1 // PART, N2, PART), jnp.float32),
@@ -283,7 +306,7 @@
         ],
         compiler_params=pltpu.CompilerParams(vmem_limit_bytes=40 * 1024 * 1024),
         name="spectrum",
-    )(where, gates, table_r, stage_one, twiddle, *pieces)
+    )(where, gates, table_r, stage_one, coarse, fine, *pieces)
 
 
 def total(array):
@@ -300,7 +323,7 @@
     own_in, rest = rest[:n_piece], rest[n_piece:]
     other_in, rest = rest[:n_piece], rest[n_piece:]
     outs, rest = rest[: plan.planes], rest[plan.planes :]
-    tmpl, psd, basis, prod, weight, inner, score, natural, blocks, acc, sem = rest
+    tmpl, psd, basis, prod, weight, inner, score, natural, blocks, acc = rest
     plane, place = where_ref[0], where_ref[1]
     freq, width, planes = plan.freq, plan.width, plan.planes
 
@@ -311,40 +334,32 @@
 
     @pl.when(plane < DET)
     def _():
-        def copy_tmpl(ref, source_plane):
+        for ahead, ref in enumerate(tmpl_in):
+            source = lax.rem(plane + ahead, planes) * width
             for m in range(width):
-                source = source_plane * width + (place ^ plan.offsets[m])
-                pltpu.make_async_copy(ref.at[m], tmpl.at[source], sem.at[0]).start()
-
-        for ahead, ref in enumerate(tmpl_in):
-            copy_tmpl(ref, lax.rem(plane + ahead, planes))
+                tmpl[source + (place ^ plan.offsets[m])] = ref[m]
+
+        def put(target, select):
+            def store(piece, f):
+                target[f] = select(piece)
+
+            return store
 
         from_pieces = functools.partial(from_plane_gather, plan, plane, place)
-        from_pieces(
-            small_in, lambda src, f: pltpu.make_async_copy(src.at[1], psd.at[f], sem.at[1]).start()
-        )
+        from_pieces(small_in, put(psd, lambda p: p[1]))
         for j in range(2):
-            from_pieces(
-                own_in,
-                lambda src, f, j=j: pltpu.make_async_copy(
-                    src.at[j], basis.at[j, f], sem.at[2]
-                ).start(),
-            )
-            from_pieces(
-                other_in,
-                lambda src, f, j=j: pltpu.make_async_copy(
-                    src.at[j], basis.at[2 + j, f], sem.at[2]
-                ).start(),
-            )
-        pltpu.make_async_copy(tmpl, tmpl, sem.at[0]).wait()
-        pltpu.make_async_copy(psd, psd, sem.at[1]).wait()
+            from_pieces(own_in, put(basis.at[j], lambda p, j=j: p[j]))
+            from_pieces(other_in, put(basis.at[2 + j], lambda p, j=j: p[j]))
+
+        chunks = PART // rows
 
         def spread_out(block, real, imag):
             tiles = [slice(a * PART, (a + 1) * PART) for a in range(RADIX_C)]
             parts = dft_eight([real[:, t] for t in tiles], [imag[:, t] for t in tiles])
+            place = lax.rem(block, chunks) * RADIX_R + lax.div(block, chunks)
             for c0, (re, im) in enumerate(parts):
                 both = jnp.concatenate([re, im], axis=1)
-                inner[c0, block] = both.astype(inner.dtype)
+                inner[c0, place] = both.astype(inner.dtype)
 
         def fold(array):
             return jnp.sum(array.reshape(rows // 8, 8, N2), axis=0)
@@ -378,21 +393,29 @@
                     c0 = 2 * cp + half
                     left = inner[c0].reshape(N1, 2 * PART).astype(jnp.bfloat16)
                     lag = jnp.dot(left, stage_one[c0], preferred_element_type=jnp.float32)
-                    g_re, g_im = lag[:, :PART], lag[:, PART:]
-                    tw_re, tw_im = twiddle[c0, :, :PART], twiddle[c0, :, PART:]
-                    y_re = g_re * tw_re - g_im * tw_im
-                    y_im = g_re * tw_im + g_im * tw_re
-                    cuts = [slice(a * PART, (a + 1) * PART) for a in range(RADIX_R)]
-                    parts = dft_four([y_re[t] for t in cuts], [y_im[t] for t in cuts])
-                    for r0, (re, im) in enumerate(parts):
-                        columns[r0].append(jnp.concatenate([re, im], axis=0).astype(jnp.bfloat16))
+                    found = [([], []) for _ in range(RADIX_R)]
+                    for q in range(chunks):
+                        y_re, y_im = [], []
+                        for a in range(RADIX_R):
+                            at = slice((q * RADIX_R + a) * rows, (q * RADIX_R + a + 1) * rows)
+                            g = lag[at, :PART], lag[at, PART:]
+                            at = slice(a * PART + q * rows, a * PART + (q + 1) * rows)
+                            tw = twiddle[c0, at, :PART], twiddle[c0, at, PART:]
+                            turned = times(g, tw)
+                            y_re.append(turned[0])
+                            y_im.append(turned[1])
+                        for r0, (re, im) in enumerate(dft_four(y_re, y_im)):
+                            found[r0][0].append(re)
+                            found[r0][1].append(im)
+                    for r0, (re, im) in enumerate(found):
+                        columns[r0].append(jnp.concatenate([*re, *im], axis=0).astype(jnp.bfloat16))
                 for r0 in range(RADIX_R):
                     right = jnp.concatenate(columns[r0], axis=1)
                     lag = jnp.dot(stage_two[r0], right, preferred_element_type=jnp.float32)
                     use(cp, r0, lag[:PART], lag[PART:])
                 return carry
 
-            lax.fori_loop(0, RADIX_C // 2, pair, 0)
+            lax.fori_loop(0, RADIX_C // 2, pair, 0, unroll=True)
 
         head_scale = 1.0 / (MODULUS * variance)
 
@@ -400,7 +423,6 @@
             score[cp, r0] = (re * re + im * im) * head_scale
 
         transforms(use_base)
-        pltpu.make_async_copy(basis, basis, sem.at[2]).wait()
 
         acc[...] = jnp.zeros_like(acc)
 
@@ -450,13 +472,12 @@
 
 def lag_scores(plan, rows, where, spectrum, tables, tmpl, small, own, other):
     vmem = pl.BlockSpec(memory_space=pltpu.VMEM)
-    hbm = pl.BlockSpec(memory_space=pl.ANY)
     streams = [*tmpl, *small, *own, *other]
     inner_type = jnp.bfloat16 if rows % 16 == 0 else jnp.float32
     return pl.pallas_call(
         functools.partial(lag_kernel, plan, rows),
         out_shape=[jax.ShapeDtypeStruct((N1, N2 // plan.planes), jnp.bfloat16)] * plan.planes,
-        in_specs=[pl.BlockSpec(memory_space=pltpu.SMEM), *[vmem] * 5, *[hbm] * len(streams)],
+        in_specs=[pl.BlockSpec(memory_space=pltpu.SMEM), *[vmem] * (5 + len(streams))],
         out_specs=[vmem] * plan.planes,
         scratch_shapes=[
             pltpu.VMEM((plan.freq, 2, rows, N2), jnp.bfloat16),
@@ -469,9 +490,8 @@
             pltpu.VMEM((RADIX_C, N1, PART), jnp.float32),
             pltpu.VMEM((plan.planes, N1, N2 // plan.planes), jnp.float32),
             pltpu.VMEM((CAL + 1, 8, N2), jnp.float32),
-            pltpu.SemaphoreType.DMA((3,)),
         ],
-        compiler_params=pltpu.CompilerParams(vmem_limit_bytes=60 * 1024 * 1024),
+        compiler_params=pltpu.CompilerParams(vmem_limit_bytes=(34 if rows % 16 == 0 else 58) * 1024 * 1024),
         name="lag_scores",
     )(where, spectrum, *tables, *streams)
 
@@ -494,16 +514,20 @@
     rings = gather_templates(plan, tmpl)
 
     small = gather_plane(plan, piece[:, :2])
-    other = lax.ppermute(piece[:, 2:], "tmpl", [(g, g ^ 1) for g in range(groups)])
+    partner = [(g, g ^ 1) for g in range(groups)]
     own = gather_plane(plan, piece[:, 2:])
-    other = gather_plane(plan, other)
+    other = [lax.ppermute(half, "tmpl", partner) for half in own[:-1]]
+    last = lax.ppermute(jnp.concatenate(other), "freq", plan.swap(plan.bits[-1]))
+    other.append(last)
 
     where = jnp.stack([plane, place]).astype(jnp.int32)
-    zero, _ = lax.optimization_barrier((jnp.int32(0), tmpl))
-    stage_one, twiddle = column_tables(zero)
+    zero = jnp.int32(0)
+    stage_one, coarse, fine = column_tables(zero)
     table_r = row_table(zero)
-    stage_two, unscramble = lag_tables(zero)
-    spectrum = spectrum_of(plan, rows, where, gate_start, table_r, stage_one, twiddle, small)
+    stage_two = lag_tables(zero)
+    spectrum, twiddle, unscramble = spectrum_of(
+        plan, rows, where, gate_start, table_r, stage_one, coarse, fine, small
+    )
     scores = lag_scores(
         plan,
         rows,

time: 162 us -> 152 us (0.938)
  the two profiles are of different devices: /device:TPU:26 before, /device:TPU:24 now
where the time goes in v1:
time: 152 us
  waiting for transfers between devices  91.3 us (60%)
  starting transfers between devices  33.4 us (22%)
  other arithmetic  16 us (11%)
  Pallas kernels  6.79 us (4%)
  local copies, waits for them, and re-layouts  4.02 us (3%)
    ppermute x3, waiting for transfers between devices, on_device(): got = lax.ppermute(scores[o], 'freq', plan.shift_out(o))  42.9 us
    ppermute x3, waiting for transfers between devices, gather_templates(): pieces.append(lax.ppermute(pieces[-1], 'freq', plan.back()))  21.9 us
    ppermute x3, starting transfers between devices, gather_templates(): pieces.append(lax.ppermute(pieces[-1], 'freq', plan.back()))  12.1 us
    ppermute x3, waiting for transfers between devices, scatter_planes(): got.append(lax.ppermute(send, 'freq', plan.shift_in(o)))  9.35 us
    ppermute x4, waiting for transfers between devices, gather_plane(): got = lax.ppermute(held, 'freq', plan.swap(b))  8.65 us
    ppermute x3, starting transfers between devices, scatter_planes(): got.append(lax.ppermute(send, 'freq', plan.shift_in(o)))  8.1 us
    ppermute x2, waiting for transfers between devices, on_device(): best = jnp.maximum(keep, lax.ppermute(send, 'freq', plan.swap(b)))  5.76 us
    another operation x3, other arithmetic  4.86 us
  transfers between devices with their start and end apart: 21, of which 12 were waited for; matrix products, arithmetic and copies ran while one was open for 11% of the time, Pallas kernels for 2%

profile of v1, /device:TPU:24, one launch (start us, length us, event | category | flops | bytes accessed | tf_op | source)
XLA Modules:
  0.0 152.0 jit_solution(16055712723827396408)
XLA Ops:
  1.2 1.6 %collective-permute-start.5 = (bf16[1,2,2,32,1024]{4,3,2,0,1:T(8,128)(2,1)S(1)}, bf16[1,2,2,32,1024]{4,3,2,0,1:T(8,128)(2,1)S(1)}, u32[]{:S(2)}, u32[]{:S(2)}) collective-permute-start(bf16[1,2,2,32,1024]{4,3,2,0,1:T(8,128)(2,1)S(1)} %get-tuple-element.27), channel_id=1, source_target_pairs={{0,2},{1,3},{2,0},{3,1},{4,6},{5,7},{6,4},{7,5},{8,10},{9,11},{10,... | collective-permute-start | bytes 786440 | tf_op jit(solution)/shard_map/ppermute | solution.py:133
  5.0 2.4 %collective-permute-start.2 = (bf16[4,32,1024]{2,1,0:T(8,128)(2,1)S(1)}, bf16[4,32,1024]{2,1,0:T(8,128)(2,1)S(1)}, u32[]{:S(2)}, u32[]{:S(2)}) collective-permute-start(bf16[4,32,1024]{2,1,0:T(8,128)(2,1)S(1)} %get-tuple-element.22), channel_id=1, source_target_pairs={{4,0},{5,1},{6,2},{7,3},{8,4},{9,5},{10,6},{11,7},{12,8},{13,9},{1... | collective-permute-start | bytes 786440 | tf_op jit(solution)/shard_map/ppermute | solution.py:114
  8.7 4.4 %collective-permute-start.1 = (bf16[4,32,1024]{2,1,0:T(8,128)(2,1)S(1)}, bf16[4,32,1024]{2,1,0:T(8,128)(2,1)S(1)}, u32[]{:S(2)}, u32[]{:S(2)}) collective-permute-start(bf16[4,32,1024]{2,1,0:T(8,128)(2,1)S(1)} %get-tuple-element.23), channel_id=1, source_target_pairs={{0,8},{1,9},{2,10},{3,11},{8,0},{9,1},{10,2},{11,3},{12,4},{13,5},... | collective-permute-start | bytes 786440 | tf_op jit(solution)/shard_map/ppermute | solution.py:114
  14.6 5.1 %collective-permute-done = bf16[4,32,1024]{2,1,0:T(8,128)(2,1)S(1)} collective-permute-done((bf16[4,32,1024]{2,1,0:T(8,128)(2,1)S(1)}, bf16[4,32,1024]{2,1,0:T(8,128)(2,1)S(1)}, u32[]{:S(2)}, u32[]{:S(2)}) %collective-permute-start) | collective-permute-done | bytes 262176 | tf_op jit(solution)/shard_map/ppermute | solution.py:114
  19.7 4.2 %collective-permute-done.1 = bf16[4,32,1024]{2,1,0:T(8,128)(2,1)S(1)} collective-permute-done((bf16[4,32,1024]{2,1,0:T(8,128)(2,1)S(1)}, bf16[4,32,1024]{2,1,0:T(8,128)(2,1)S(1)}, u32[]{:S(2)}, u32[]{:S(2)}) %collective-permute-start.1) | collective-permute-done | bytes 262176 | tf_op jit(solution)/shard_map/ppermute | solution.py:114
  25.9 1.6 %collective-permute-start.12 = (bf16[1,4,2,32,1024]{4,3,2,1,0:T(8,128)(2,1)S(1)}, bf16[1,4,2,32,1024]{4,3,2,1,0:T(8,128)(2,1)S(1)}, u32[]{:S(2)}, u32[]{:S(2)}) collective-permute-start(bf16[1,4,2,32,1024]{4,3,2,1,0:T(8,128)(2,1)S(1)} %get-tuple-element.19.rest_7_), channel_id=1, source_target_pairs={{0,16},{16,0},{1,17},{17,1},{2,18},{18,2},{3,19},{19,3},{4,20},{20... | collective-permute-start | bytes 1572872 | tf_op jit(solution)/shard_map/ppermute | solution.py:519
  27.5 1.5 collective-permute-start.3
  29.1 6.1 %collective-permute-start.7 = (bf16[4,2,32,1024]{3,2,1,0:T(8,128)(2,1)S(1)}, bf16[4,2,32,1024]{3,2,1,0:T(8,128)(2,1)S(1)}, u32[]{:S(2)}, u32[]{:S(2)}) collective-permute-start(bf16[4,2,32,1024]{3,2,1,0:T(8,128)(2,1)S(1)} %maximum_bitcast_fusion.rest_0_), channel_id=1, source_target_pairs={{0,12},{1,13},{2,14},{3,15},{4,0},{5,1},{6,2},{7,3},{8,4},{9,5},{1... | collective-permute-start | bytes 1572872 | tf_op jit(solution)/shard_map/ppermute | solution.py:141
  35.2 3.8 %collective-permute-done.10.rest_8_ = bf16[1,4,2,32,1024]{4,3,2,1,0:T(8,128)(2,1)S(1)} collective-permute-done((bf16[1,4,2,32,1024]{4,3,2,1,0:T(8,128)(2,1)S(1)}, bf16[1,4,2,32,1024]{4,3,2,1,0:T(8,128)(2,1)S(1)}, u32[]{:S(2)}, u32[]{:S(2)}) %collective-permute-start.10) | collective-permute-done | bytes 524320 | tf_op jit(solution)/shard_map/ppermute | solution.py:122
  39.0 1.5 collective-permute-start.13
  43.1 4.8 %collective-permute-done.3.rest_1_.rest_5_ = bf16[1,4,2,32,1024]{4,3,2,1,0:T(8,128)(2,1)S(1)} collective-permute-done((bf16[1,4,2,32,1024]{4,3,2,1,0:T(8,128)(2,1)S(1)}, bf16[1,4,2,32,1024]{4,3,2,1,0:T(8,128)(2,1)S(1)}, u32[]{:S(2)}, u32[]{:S(2)}) %collective-permute-start.3) | collective-permute-done | bytes 524320 | tf_op jit(solution)/shard_map/ppermute | solution.py:122
  50.0 6.1 %collective-permute-start.8 = (bf16[4,2,32,1024]{3,2,1,0:T(8,128)(2,1)S(1)}, bf16[4,2,32,1024]{3,2,1,0:T(8,128)(2,1)}, u32[]{:S(2)}, u32[]{:S(2)}) collective-permute-start(bf16[4,2,32,1024]{3,2,1,0:T(8,128)(2,1)S(1)} %collective-permute-done.7.rest_1_), channel_id=1, source_target_pairs={{0,12},{1,13},{2,14},{3,15},{4,0},{5,1},{6,2},{7,3},{8,4},{9,5},{1... | collective-permute-start | bytes 1572872 | tf_op jit(solution)/shard_map/ppermute | solution.py:141
  58.4 1.4 subtract_convert_fusion
  59.7 11.8 %collective-permute-done.8.rest_2_ = bf16[4,2,32,1024]{3,2,1,0:T(8,128)(2,1)} collective-permute-done((bf16[4,2,32,1024]{3,2,1,0:T(8,128)(2,1)S(1)}, bf16[4,2,32,1024]{3,2,1,0:T(8,128)(2,1)}, u32[]{:S(2)}, u32[]{:S(2)}) %collective-permute-start.8) | collective-permute-done | bytes 524320 | tf_op jit(solution)/shard_map/ppermute | solution.py:141
  73.0 2.2 %fusion.14 = (bf16[8,128,128]{2,1,0:T(8,128)(2,1)S(1)}, bf16[8,128,128]{2,1,0:T(8,128)(2,1)S(1)}, bf16[8,128,128]{2,1,0:T(8,128)(2,1)S(1)}) fusion(s32[8,128]{1,0:T(8,128)S(1)} %iota_add_fusion), kind=kLoop, calls=%fused_computation.48 | loop fusion | flops 2359296 | bytes 790528 | tf_op jit(solution)/shard_map/convert.11
  75.5 2.6 %spectrum.1 = (f32[2,512,1024]{2,1,0:T(8,128)S(1)}, f32[8,512,256]{2,1,0:T(8,128)}, bf16[1024,1024]{1,0:T(8,128)(2,1)S(1)}) custom-call(s32[2]{0:T(128)S(1)} %pad_add_fusion.where_ref, s32[3,2]{1,0:T(4,128)S(1)} %copy.6.gates_ref, bf16[1024,512]{1,0:T(8,128)(2,1)S(1)} %pad_maximum_fusion.row_table_ref, ...), custom_call_target="tpu_custom_call" | custom-call | tf_op jit(solution)/shard_map/spectrum/pallas_call | solution.py:292
  78.0 9.3 %collective-permute-done.9.rest_3_ = bf16[4,2,32,1024]{3,2,1,0:T(8,128)(2,1)} collective-permute-done((bf16[4,2,32,1024]{3,2,1,0:T(8,128)(2,1)}, bf16[4,2,32,1024]{3,2,1,0:T(8,128)(2,1)}, u32[]{:S(2)}, u32[]{:S(2)}) %collective-permute-start.9) | collective-permute-done | bytes 524320 | tf_op jit(solution)/shard_map/ppermute | solution.py:141
  87.4 4.2 %lag_scores.1 = (bf16[512,256]{1,0:T(8,128)(2,1)S(1)}, bf16[512,256]{1,0:T(8,128)(2,1)}, bf16[512,256]{1,0:T(8,128)(2,1)}, bf16[512,256]{1,0:T(8,128)(2,1)}) custom-call(s32[2]{0:T(128)S(1)} %pad_add_fusion.where_ref, f32[2,512,1024]{2,1,0:T(8,128)S(1)} %get-tuple-element.12.spectrum, bf16[8,256,256]{2,1,0:T(8,128)(2,1)S(1)} %maximum_maximum_fusion.stage_one, ...), custom_call_target="tpu_custom_call" | custom-call | tf_op jit(solution)/shard_map/lag_scores/pallas_call | solution.py:477
  96.2 24.0 %collective-permute-done.15 = bf16[512,256]{1,0:T(8,128)(2,1)S(1)} collective-permute-done((bf16[512,256]{1,0:T(8,128)(2,1)}, bf16[512,256]{1,0:T(8,128)(2,1)S(1)}, u32[]{:S(2)}, u32[]{:S(2)}) %collective-permute-start.15) | collective-permute-done | bytes 262176 | tf_op jit(solution)/shard_map/ppermute | solution.py:545
  120.2 18.9 %collective-permute-done.16 = bf16[512,256]{1,0:T(8,128)(2,1)S(1)} collective-permute-done((bf16[512,256]{1,0:T(8,128)(2,1)}, bf16[512,256]{1,0:T(8,128)(2,1)S(1)}, u32[]{:S(2)}, u32[]{:S(2)}) %collective-permute-start.16) | collective-permute-done | bytes 262176 | tf_op jit(solution)/shard_map/ppermute | solution.py:545
  140.7 4.4 %collective-permute-done.18 = bf16[512,128]{1,0:T(8,128)(2,1)S(1)} collective-permute-done((bf16[512,128]{1,0:T(8,128)(2,1)S(1)}, bf16[512,128]{1,0:T(8,128)(2,1)S(1)}, u32[]{:S(2)}, u32[]{:S(2)}) %collective-permute-start.18) | collective-permute-done | bytes 131104 | tf_op jit(solution)/shard_map/ppermute | solution.py:553
  145.4 1.3 collective-permute-done.19
  146.9 1.6 %collective-permute-start.20 = (bf16[256,64]{1,0:T(8,128)(2,1)S(1)}, bf16[256,64]{1,0:T(8,128)(2,1)S(1)}, u32[]{:S(2)}, u32[]{:S(2)}) collective-permute-start(bf16[256,64]{1,0:T(8,128)(2,1)S(1)} %constant_dynamic-slice_fusion), channel_id=1, source_target_pairs={{0,16},{16,0},{1,17},{17,1},{2,18},{18,2},{3,19},{19,3},{4,20},{20... | collective-permute-start | bytes 98312 | tf_op jit(solution)/shard_map/ppermute | solution.py:561
  148.5 2.7 %collective-permute-done.20 = bf16[256,64]{1,0:T(8,128)(2,1)S(1)} collective-permute-done((bf16[256,64]{1,0:T(8,128)(2,1)S(1)}, bf16[256,64]{1,0:T(8,128)(2,1)S(1)}, u32[]{:S(2)}, u32[]{:S(2)}) %collective-permute-start.20) | collective-permute-done | bytes 32800 | tf_op jit(solution)/shard_map/ppermute | solution.py:561
  (95 shorter events, 24.0 us)
Async XLA Ops:
  1.2 23.6 %collective-permute-start.5 = (bf16[1,2,2,32,1024]{4,3,2,0,1:T(8,128)(2,1)S(1)}, bf16[1,2,2,32,1024]{4,3,2,0,1:T(8,128)(2,1)S(1)}, u32[]{:S(2)}, u32[]{:S(2)}) collective-permute-start(bf16[1,2,2,32,1024]{4,3,2,0,1:T(8,128)(2,1)S(1)} %get-tuple-element.27), channel_id=1, source_target_pairs={{0,2},{1,3},{2,0},{3,1},{4,6},{5,7},{6,4},{7,5},{8,10},{9,11},{10,... | collective-permute-start | bytes 786440 | tf_op jit(solution)/shard_map/ppermute | solution.py:133
  5.0 9.6 %collective-permute-start.2 = (bf16[4,32,1024]{2,1,0:T(8,128)(2,1)S(1)}, bf16[4,32,1024]{2,1,0:T(8,128)(2,1)S(1)}, u32[]{:S(2)}, u32[]{:S(2)}) collective-permute-start(bf16[4,32,1024]{2,1,0:T(8,128)(2,1)S(1)} %get-tuple-element.22), channel_id=1, source_target_pairs={{4,0},{5,1},{6,2},{7,3},{8,4},{9,5},{10,6},{11,7},{12,8},{13,9},{1... | collective-permute-start | bytes 786440 | tf_op jit(solution)/shard_map/ppermute | solution.py:114
  7.4 12.3 %collective-permute-start = (bf16[4,32,1024]{2,1,0:T(8,128)(2,1)S(1)}, bf16[4,32,1024]{2,1,0:T(8,128)(2,1)S(1)}, u32[]{:S(2)}, u32[]{:S(2)}) collective-permute-start(bf16[4,32,1024]{2,1,0:T(8,128)(2,1)S(1)} %get-tuple-element.24), channel_id=1, source_target_pairs={{0,4},{1,5},{2,6},{3,7},{4,8},{5,9},{6,10},{7,11},{12,0},{13,1},{1... | collective-permute-start | bytes 786440 | tf_op jit(solution)/shard_map/ppermute | solution.py:114
  8.7 15.2 %collective-permute-start.1 = (bf16[4,32,1024]{2,1,0:T(8,128)(2,1)S(1)}, bf16[4,32,1024]{2,1,0:T(8,128)(2,1)S(1)}, u32[]{:S(2)}, u32[]{:S(2)}) collective-permute-start(bf16[4,32,1024]{2,1,0:T(8,128)(2,1)S(1)} %get-tuple-element.23), channel_id=1, source_target_pairs={{0,8},{1,9},{2,10},{3,11},{8,0},{9,1},{10,2},{11,3},{12,4},{13,5},... | collective-permute-start | bytes 786440 | tf_op jit(solution)/shard_map/ppermute | solution.py:114
  24.1 14.9 %collective-permute-start.10 = (bf16[1,4,2,32,1024]{4,3,2,1,0:T(8,128)(2,1)S(1)}, bf16[1,4,2,32,1024]{4,3,2,1,0:T(8,128)(2,1)S(1)}, u32[]{:S(2)}, u32[]{:S(2)}) collective-permute-start(bf16[1,4,2,32,1024]{4,3,2,1,0:T(8,128)(2,1)S(1)} %get-tuple-element.19.rest_7_), channel_id=1, source_target_pairs={{0,2},{1,3},{2,0},{3,1},{4,6},{5,7},{6,4},{7,5},{8,10},{9,11},{10,... | collective-permute-start | bytes 1572872 | tf_op jit(solution)/shard_map/ppermute | solution.py:122
  24.8 4.2 %collective-permute-start.6 = (bf16[2,1,2,32,1024]{4,3,2,0,1:T(8,128)(2,1)S(1)}, bf16[2,1,2,32,1024]{4,3,2,0,1:T(8,128)(2,1)S(1)}, u32[]{:S(2)}, u32[]{:S(2)}) collective-permute-start(bf16[2,1,2,32,1024]{4,3,2,0,1:T(8,128)(2,1)S(1)} %get-tuple-element.26), channel_id=1, source_target_pairs={{0,1},{1,0},{2,3},{3,2},{4,5},{5,4},{6,7},{7,6},{8,9},{9,8},{10,11... | collective-permute-start | bytes 786440 | tf_op jit(solution)/shard_map/ppermute | solution.py:133
  25.9 30.1 %collective-permute-start.12 = (bf16[1,4,2,32,1024]{4,3,2,1,0:T(8,128)(2,1)S(1)}, bf16[1,4,2,32,1024]{4,3,2,1,0:T(8,128)(2,1)S(1)}, u32[]{:S(2)}, u32[]{:S(2)}) collective-permute-start(bf16[1,4,2,32,1024]{4,3,2,1,0:T(8,128)(2,1)S(1)} %get-tuple-element.19.rest_7_), channel_id=1, source_target_pairs={{0,16},{16,0},{1,17},{17,1},{2,18},{18,2},{3,19},{19,3},{4,20},{20... | collective-permute-start | bytes 1572872 | tf_op jit(solution)/shard_map/ppermute | solution.py:519
  27.5 20.4 %collective-permute-start.3 = (bf16[1,4,2,32,1024]{4,3,2,1,0:T(8,128)(2,1)S(1)}, bf16[1,4,2,32,1024]{4,3,2,1,0:T(8,128)(2,1)S(1)}, u32[]{:S(2)}, u32[]{:S(2)}) collective-permute-start(bf16[1,4,2,32,1024]{4,3,2,1,0:T(8,128)(2,1)S(1)} %get-tuple-element.20.rest_0_.rest_4_), channel_id=1, source_target_pairs={{0,2},{1,3},{2,0},{3,1},{4,6},{5,7},{6,4},{7,5},{8,10},{9,11},{10,... | collective-permute-start | bytes 1572872 | tf_op jit(solution)/shard_map/ppermute | solution.py:122
  29.1 20.0 %copy-start.2 = (bf16[4,2,32,1024]{3,2,1,0:T(8,128)(2,1)}, bf16[4,2,32,1024]{3,2,1,0:T(8,128)(2,1)S(1)}, u32[]{:S(2)}) copy-start(bf16[4,2,32,1024]{3,2,1,0:T(8,128)(2,1)S(1)} %maximum_bitcast_fusion.rest_0_) | copy-start | bytes 1572868
  29.1 20.9 %collective-permute-start.7 = (bf16[4,2,32,1024]{3,2,1,0:T(8,128)(2,1)S(1)}, bf16[4,2,32,1024]{3,2,1,0:T(8,128)(2,1)S(1)}, u32[]{:S(2)}, u32[]{:S(2)}) collective-permute-start(bf16[4,2,32,1024]{3,2,1,0:T(8,128)(2,1)S(1)} %maximum_bitcast_fusion.rest_0_), channel_id=1, source_target_pairs={{0,12},{1,13},{2,14},{3,15},{4,0},{5,1},{6,2},{7,3},{8,4},{9,5},{1... | collective-permute-start | bytes 1572872 | tf_op jit(solution)/shard_map/ppermute | solution.py:141
  39.0 17.1 %collective-permute-start.13 = (bf16[1,4,2,32,1024]{4,3,2,1,0:T(8,128)(2,1)S(1)}, bf16[1,4,2,32,1024]{4,3,2,1,0:T(8,128)(2,1)S(1)}, u32[]{:S(2)}, u32[]{:S(2)}) collective-permute-start(bf16[1,4,2,32,1024]{4,3,2,1,0:T(8,128)(2,1)S(1)} %collective-permute-done.10.rest_8_), channel_id=1, source_target_pairs={{0,16},{16,0},{1,17},{17,1},{2,18},{18,2},{3,19},{19,3},{4,20},{20... | collective-permute-start | bytes 1572872 | tf_op jit(solution)/shard_map/ppermute | solution.py:519
  43.1 34.9 %collective-permute-start.11 = (bf16[2,4,2,32,1024]{4,3,2,1,0:T(8,128)(2,1)}, bf16[2,4,2,32,1024]{4,3,2,1,0:T(8,128)(2,1)}, u32[]{:S(2)}, u32[]{:S(2)}) collective-permute-start(bf16[2,4,2,32,1024]{4,3,2,1,0:T(8,128)(2,1)} %pad_maximum_fusion.3), channel_id=1, source_target_pairs={{0,1},{1,0},{2,3},{3,2},{4,5},{5,4},{6,7},{7,6},{8,9},{9,8},{10,11... | collective-permute-start | bytes 3145736 | tf_op jit(solution)/shard_map/ppermute | solution.py:122
  49.1 22.5 %copy-start.16 = (s32[3,2]{0,1:T(2,128)S(1)}, s32[3,2]{0,1:T(2,128)}, u32[]{:S(2)}) copy-start(s32[3,2]{0,1:T(2,128)} %param.6) | copy-start | bytes 76
  49.1 26.4 %collective-permute-start.4 = (bf16[2,4,2,32,1024]{4,3,2,1,0:T(8,128)(2,1)}, bf16[2,4,2,32,1024]{4,3,2,1,0:T(8,128)(2,1)S(1)}, u32[]{:S(2)}, u32[]{:S(2)}) collective-permute-start(bf16[2,4,2,32,1024]{4,3,2,1,0:T(8,128)(2,1)} %pad_maximum_fusion.2), channel_id=1, source_target_pairs={{0,1},{1,0},{2,3},{3,2},{4,5},{5,4},{6,7},{7,6},{8,9},{9,8},{10,11... | collective-permute-start | bytes 3145736 | tf_op jit(solution)/shard_map/ppermute | solution.py:122
  50.0 21.5 %collective-permute-start.8 = (bf16[4,2,32,1024]{3,2,1,0:T(8,128)(2,1)S(1)}, bf16[4,2,32,1024]{3,2,1,0:T(8,128)(2,1)}, u32[]{:S(2)}, u32[]{:S(2)}) collective-permute-start(bf16[4,2,32,1024]{3,2,1,0:T(8,128)(2,1)S(1)} %collective-permute-done.7.rest_1_), channel_id=1, source_target_pairs={{0,12},{1,13},{2,14},{3,15},{4,0},{5,1},{6,2},{7,3},{8,4},{9,5},{1... | collective-permute-start | bytes 1572872 | tf_op jit(solution)/shard_map/ppermute | solution.py:141
  57.3 30.0 %collective-permute-start.14 = (bf16[2,4,2,32,1024]{4,3,2,1,0:T(8,128)(2,1)}, bf16[2,4,2,32,1024]{4,3,2,1,0:T(8,128)(2,1)}, u32[]{:S(2)}, u32[]{:S(2)}) collective-permute-start(bf16[2,4,2,32,1024]{4,3,2,1,0:T(8,128)(2,1)} %pad_maximum_fusion.4), channel_id=1, source_target_pairs={{0,1},{1,0},{2,3},{3,2},{4,5},{5,4},{6,7},{7,6},{8,9},{9,8},{10,11... | collective-permute-start | bytes 3145736 | tf_op jit(solution)/shard_map/ppermute | solution.py:520
  71.5 15.8 %collective-permute-start.9 = (bf16[4,2,32,1024]{3,2,1,0:T(8,128)(2,1)}, bf16[4,2,32,1024]{3,2,1,0:T(8,128)(2,1)}, u32[]{:S(2)}, u32[]{:S(2)}) collective-permute-start(bf16[4,2,32,1024]{3,2,1,0:T(8,128)(2,1)} %collective-permute-done.8.rest_2_), channel_id=1, source_target_pairs={{0,12},{1,13},{2,14},{3,15},{4,0},{5,1},{6,2},{7,3},{8,4},{9,5},{1... | collective-permute-start | bytes 1572872 | tf_op jit(solution)/shard_map/ppermute | solution.py:141
  75.4 11.9 %copy-start.1 = (bf16[4,256,256]{2,1,0:T(8,128)(2,1)S(1)}, bf16[4,256,256]{2,1,0:T(8,128)(2,1)}, u32[]{:S(2)}) copy-start(bf16[4,256,256]{2,1,0:T(8,128)(2,1)} %maximum_maximum_fusion.1.stage_two) | copy-start | bytes 1572868
  92.3 27.9 %collective-permute-start.15 = (bf16[512,256]{1,0:T(8,128)(2,1)}, bf16[512,256]{1,0:T(8,128)(2,1)S(1)}, u32[]{:S(2)}, u32[]{:S(2)}) collective-permute-start(bf16[512,256]{1,0:T(8,128)(2,1)} %get-tuple-element.16), channel_id=1, source_target_pairs={{0,4},{1,5},{2,6},{3,7},{4,8},{5,9},{6,10},{7,11},{8,12},{9,13},{1... | collective-permute-start | bytes 786440 | tf_op jit(solution)/shard_map/ppermute | solution.py:545
  93.6 45.5 %collective-permute-start.16 = (bf16[512,256]{1,0:T(8,128)(2,1)}, bf16[512,256]{1,0:T(8,128)(2,1)S(1)}, u32[]{:S(2)}, u32[]{:S(2)}) collective-permute-start(bf16[512,256]{1,0:T(8,128)(2,1)} %get-tuple-element.17), channel_id=1, source_target_pairs={{0,8},{1,9},{2,10},{3,11},{4,12},{5,13},{6,14},{7,15},{8,0},{9,1},... | collective-permute-start | bytes 786440 | tf_op jit(solution)/shard_map/ppermute | solution.py:545
  94.9 44.2 %collective-permute-start.17 = (bf16[512,256]{1,0:T(8,128)(2,1)}, bf16[512,256]{1,0:T(8,128)(2,1)S(1)}, u32[]{:S(2)}, u32[]{:S(2)}) collective-permute-start(bf16[512,256]{1,0:T(8,128)(2,1)} %get-tuple-element.18), channel_id=1, source_target_pairs={{0,12},{1,13},{2,14},{3,15},{4,0},{5,1},{6,2},{7,3},{8,4},{9,5},{1... | collective-permute-start | bytes 786440 | tf_op jit(solution)/shard_map/ppermute | solution.py:545
  140.2 5.0 %collective-permute-start.18 = (bf16[512,128]{1,0:T(8,128)(2,1)S(1)}, bf16[512,128]{1,0:T(8,128)(2,1)S(1)}, u32[]{:S(2)}, u32[]{:S(2)}) collective-permute-start(bf16[512,128]{1,0:T(8,128)(2,1)S(1)} %constant_dynamic-slice_fusion.2), channel_id=1, source_target_pairs={{0,2},{1,3},{2,0},{3,1},{4,6},{5,7},{6,4},{7,5},{8,10},{9,11},{10,... | collective-permute-start | bytes 393224 | tf_op jit(solution)/shard_map/ppermute | solution.py:553
  145.3 1.4 collective-permute-start.19
  146.9 4.3 %collective-permute-start.20 = (bf16[256,64]{1,0:T(8,128)(2,1)S(1)}, bf16[256,64]{1,0:T(8,128)(2,1)S(1)}, u32[]{:S(2)}, u32[]{:S(2)}) collective-permute-start(bf16[256,64]{1,0:T(8,128)(2,1)S(1)} %constant_dynamic-slice_fusion), channel_id=1, source_target_pairs={{0,16},{16,0},{1,17},{17,1},{2,18},{18,2},{3,19},{19,3},{4,20},{20... | collective-permute-start | bytes 98312 | tf_op jit(solution)/shard_map/ppermute | solution.py:561
  (14 other events, 114.5 us)

commit v2 on v1

--- a/solution.py
+++ b/solution.py
@@ -115,14 +115,19 @@
     return jnp.stack(got)
 
 
-def gather_plane(plan, piece):
+def spread_plane(plan, piece):
     held = piece[None]
     pieces = [held]
-    for b in plan.bits:
+    for i, b in enumerate(plan.bits[:-1]):
         got = lax.ppermute(held, "freq", plan.swap(b))
         pieces.append(got)
-        held = jnp.concatenate([held, got])
+        held = jnp.concatenate(pieces) if i + 2 < len(plan.bits) else None
     return pieces
+
+
+def swap_last(plan, pieces):
+    swap = plan.swap(plan.bits[-1])
+    return [lax.ppermute(p, "freq", swap) for p in pieces]
 
 
 def scatter_templates(plan, place, templates):
@@ -200,7 +205,7 @@
 def spectrum_kernel(
     plan, rows, where_ref, gates_ref, row_table_ref, stage_one, coarse_ref, fine_ref, *rest
 ):
-    pieces, rest = rest[: 1 + len(plan.bits)], rest[1 + len(plan.bits) :]
+    pieces, rest = rest[:-7], rest[-7:]
     out, twiddle, unscramble, blocks, samples, parts, sem = rest
     plane, place = where_ref[0], where_ref[1]
 
@@ -304,7 +309,7 @@
             pltpu.VMEM((RADIX_C, N1, 2 * PART), jnp.float32),
             pltpu.SemaphoreType.DMA,
         ],
-        compiler_params=pltpu.CompilerParams(vmem_limit_bytes=40 * 1024 * 1024),
+        compiler_params=pltpu.CompilerParams(vmem_limit_bytes=(26 if rows % 16 == 0 else 40) * 1024 * 1024),
         name="spectrum",
     )(where, gates, table_r, stage_one, coarse, fine, *pieces)
 
@@ -317,11 +322,11 @@
     plan, rows, where_ref, spectrum, stage_one, stage_two, twiddle, unscramble, *rest
 ):
     n_tmpl = plan.planes
-    n_piece = 1 + len(plan.bits)
     tmpl_in, rest = rest[:n_tmpl], rest[n_tmpl:]
-    small_in, rest = rest[:n_piece], rest[n_piece:]
-    own_in, rest = rest[:n_piece], rest[n_piece:]
-    other_in, rest = rest[:n_piece], rest[n_piece:]
+    small_in, rest = rest[:4], rest[4:]
+    own_in, rest = rest[:4], rest[4:]
+    near_in, rest = rest[:2], rest[2:]
+    far_in, rest = rest[:4], rest[4:]
     outs, rest = rest[: plan.planes], rest[plan.planes :]
     tmpl, psd, basis, prod, weight, inner, score, natural, blocks, acc = rest
     plane, place = where_ref[0], where_ref[1]
@@ -349,7 +354,9 @@
         from_pieces(small_in, put(psd, lambda p: p[1]))
         for j in range(2):
             from_pieces(own_in, put(basis.at[j], lambda p, j=j: p[j]))
-            from_pieces(other_in, put(basis.at[2 + j], lambda p, j=j: p[j]))
+            others = [near_in[0].at[:, :, pl.ds(j, 1)], far_in[j]]
+            others += [near_in[1].at[:, :, pl.ds(j, 1)], far_in[2 + j]]
+            from_pieces(others, put(basis.at[2 + j], lambda p: p[0]))
 
         chunks = PART // rows
 
@@ -470,9 +477,9 @@
             ref[...] = blocks[lax.rem(plane + o, planes)].astype(jnp.bfloat16)
 
 
-def lag_scores(plan, rows, where, spectrum, tables, tmpl, small, own, other):
+def lag_scores(plan, rows, where, spectrum, tables, tmpl, small, own, near, far):
     vmem = pl.BlockSpec(memory_space=pltpu.VMEM)
-    streams = [*tmpl, *small, *own, *other]
+    streams = [*tmpl, *small, *own, *near, *far]
     inner_type = jnp.bfloat16 if rows % 16 == 0 else jnp.float32
     return pl.pallas_call(
         functools.partial(lag_kernel, plan, rows),
@@ -513,12 +520,18 @@
     tmpl = scatter_templates(plan, place, templates)
     rings = gather_templates(plan, tmpl)
 
-    small = gather_plane(plan, piece[:, :2])
+    small = spread_plane(plan, piece[:, :2])
+    small = small + swap_last(plan, small)
     partner = [(g, g ^ 1) for g in range(groups)]
-    own = gather_plane(plan, piece[:, 2:])
-    other = [lax.ppermute(half, "tmpl", partner) for half in own[:-1]]
-    last = lax.ppermute(jnp.concatenate(other), "freq", plan.swap(plan.bits[-1]))
-    other.append(last)
+    own = spread_plane(plan, piece[:, 2:])
+    near = [lax.ppermute(own[0], "tmpl", partner)]
+    far = [
+        lax.ppermute(near[0][:, :, :1], "freq", plan.swap(plan.bits[0])),
+        lax.ppermute(own[1][:, :, 1:], "tmpl", partner),
+    ]
+    own = own + swap_last(plan, own)
+    near = near + swap_last(plan, near)
+    far = far + swap_last(plan, far)
 
     where = jnp.stack([plane, place]).astype(jnp.int32)
     zero = jnp.int32(0)
@@ -537,7 +550,8 @@
         rings,
         small,
         own,
-        other,
+        near,
+        far,
     )
 
     summed = scores[0].astype(jnp.float32)

time: 152 us -> 148 us (0.974)
  starting transfers between devices: 33.4 us -> 27.6 us
  local copies, waits for them, and re-layouts: 4.02 us -> 9.33 us
  other arithmetic: 16 us -> 11.6 us
  waiting for transfers between devices: 91.3 us -> 93.9 us
  Pallas kernels: 6.79 us -> 4.19 us
    ppermute x3, waiting for transfers between devices: 21.9 us -> 14.3 us  [gather_templates(): pieces.append(lax.ppermute(pieces[-1], 'freq', plan.back()))]
    ppermute x7 -> x12, waiting for transfers between devices: 8.66 us -> 15.6 us  [the longest x2 9.22 us: spread_plane(): got = lax.ppermute(held, 'freq', plan.swap(b))]
    ppermute x3, starting transfers between devices: 12.1 us -> 6.44 us  [gather_templates(): pieces.append(lax.ppermute(pieces[-1], 'freq', plan.back()))]
    ppermute x3, waiting for transfers between devices: 42.9 us -> 48.4 us  [on_device(): got = lax.ppermute(scores[o], 'freq', plan.shift_out(o))]
    concatenate x3 -> x0, other arithmetic: 3.37 us -> none  [the longest x2 2.15 us: gather_plane(): held = jnp.concatenate([held, got])]
    ppermute x3, waiting for transfers between devices: 9.35 us -> 6.16 us  [scatter_planes(): got.append(lax.ppermute(send, 'freq', plan.shift_in(o)))]
    unnamed x35 -> x33, local copies, waits for them, and re-layouts: 0.85 us -> 3.52 us
    slice x0 -> x2, local copies, waits for them, and re-layouts: none -> 2.64 us  [the longest x1 1.67 us: on_device(): own[1][:, :, 1:]]
  transfers between devices with their start and end apart: 21 -> 26, of which waited for: 12 -> 13; matrix products, arithmetic and copies ran while one was open for 11% -> 10% of each run, Pallas kernels for 2% -> 0%
where the time goes in v2:
time: 148 us; the launch traced here: 147 us
  waiting for transfers between devices  93.9 us (63%)
  starting transfers between devices  27.6 us (19%)
  other arithmetic  11.6 us (8%)
  local copies, waits for them, and re-layouts  9.33 us (6%)
  Pallas kernels  4.19 us (3%)
    ppermute x3, waiting for transfers between devices, on_device(): got = lax.ppermute(scores[o], 'freq', plan.shift_out(o))  48.4 us
    ppermute x3, waiting for transfers between devices, gather_templates(): pieces.append(lax.ppermute(pieces[-1], 'freq', plan.back()))  14.3 us
    ppermute x2, waiting for transfers between devices, spread_plane(): got = lax.ppermute(held, 'freq', plan.swap(b))  9.22 us
    ppermute x3, starting transfers between devices, scatter_planes(): got.append(lax.ppermute(send, 'freq', plan.shift_in(o)))  8.79 us
    ppermute x3, starting transfers between devices, gather_templates(): pieces.append(lax.ppermute(pieces[-1], 'freq', plan.back()))  6.44 us
    ppermute x3, waiting for transfers between devices, scatter_planes(): got.append(lax.ppermute(send, 'freq', plan.shift_in(o)))  6.16 us
    ppermute x2, waiting for transfers between devices, on_device(): best = jnp.maximum(keep, lax.ppermute(send, 'freq', plan.swap(b)))  5.75 us
    another operation x3, other arithmetic  5.51 us
  transfers between devices with their start and end apart: 26, of which 13 were waited for; matrix products, arithmetic and copies ran while one was open for 10% of the time, Pallas kernels for 0%

profile of v2, /device:TPU:24, one launch (start us, length us, event | category | flops | bytes accessed | tf_op | source)
XLA Modules:
  0.0 147.2 jit_solution(18087944128970605875)
XLA Ops:
  1.2 1.6 %collective-permute-start.6 = (bf16[1,2,2,32,1024]{4,3,2,0,1:T(8,128)(2,1)S(1)}, bf16[1,2,2,32,1024]{4,3,2,0,1:T(8,128)(2,1)S(1)}, u32[]{:S(2)}, u32[]{:S(2)}) collective-permute-start(bf16[1,2,2,32,1024]{4,3,2,0,1:T(8,128)(2,1)S(1)} %get-tuple-element.27), channel_id=1, source_target_pairs={{0,2},{1,3},{2,0},{3,1},{4,6},{5,7},{6,4},{7,5},{8,10},{9,11},{10,... | collective-permute-start | bytes 786440 | tf_op jit(solution)/shard_map/ppermute | solution.py:138
  5.0 2.4 %collective-permute-start.2 = (bf16[4,32,1024]{2,1,0:T(8,128)(2,1)S(1)}, bf16[4,32,1024]{2,1,0:T(8,128)(2,1)S(1)}, u32[]{:S(2)}, u32[]{:S(2)}) collective-permute-start(bf16[4,32,1024]{2,1,0:T(8,128)(2,1)S(1)} %get-tuple-element.22), channel_id=1, source_target_pairs={{4,0},{5,1},{6,2},{7,3},{8,4},{9,5},{10,6},{11,7},{12,8},{13,9},{1... | collective-permute-start | bytes 786440 | tf_op jit(solution)/shard_map/ppermute | solution.py:114
  8.7 5.1 %collective-permute-start.1 = (bf16[4,32,1024]{2,1,0:T(8,128)(2,1)S(1)}, bf16[4,32,1024]{2,1,0:T(8,128)(2,1)}, u32[]{:S(2)}, u32[]{:S(2)}) collective-permute-start(bf16[4,32,1024]{2,1,0:T(8,128)(2,1)S(1)} %get-tuple-element.23), channel_id=1, source_target_pairs={{0,8},{1,9},{2,10},{3,11},{8,0},{9,1},{10,2},{11,3},{12,4},{13,5},... | collective-permute-start | bytes 786440 | tf_op jit(solution)/shard_map/ppermute | solution.py:114
  14.3 1.4 subtract_convert_fusion
  15.7 1.9 %negate_convert_fusion.2 = (bf16[4,128,128]{2,1,0:T(8,128)(2,1)}, bf16[4,128,128]{2,1,0:T(8,128)(2,1)}, bf16[4,128,128]{2,1,0:T(8,128)(2,1)}) fusion(s32[4,128]{1,0:T(4,128)S(1)} %iota_add_fusion.1), kind=kLoop, calls=%fused_computation.37 | loop fusion | flops 1179648 | bytes 395264 | tf_op jit(solution)/shard_map/convert.5
  17.7 2.0 %collective-permute-done = bf16[4,32,1024]{2,1,0:T(8,128)(2,1)S(1)} collective-permute-done((bf16[4,32,1024]{2,1,0:T(8,128)(2,1)S(1)}, bf16[4,32,1024]{2,1,0:T(8,128)(2,1)S(1)}, u32[]{:S(2)}, u32[]{:S(2)}) %collective-permute-start) | collective-permute-done | bytes 262176 | tf_op jit(solution)/shard_map/ppermute | solution.py:114
  19.7 4.2 %collective-permute-done.1 = bf16[4,32,1024]{2,1,0:T(8,128)(2,1)} collective-permute-done((bf16[4,32,1024]{2,1,0:T(8,128)(2,1)S(1)}, bf16[4,32,1024]{2,1,0:T(8,128)(2,1)}, u32[]{:S(2)}, u32[]{:S(2)}) %collective-permute-start.1) | collective-permute-done | bytes 262176 | tf_op jit(solution)/shard_map/ppermute | solution.py:114
  25.1 1.6 %collective-permute-start.14 = (bf16[1,4,2,32,1024]{4,3,2,1,0:T(8,128)(2,1)S(1)}, bf16[1,4,2,32,1024]{4,3,2,1,0:T(8,128)(2,1)}, u32[]{:S(2)}, u32[]{:S(2)}) collective-permute-start(bf16[1,4,2,32,1024]{4,3,2,1,0:T(8,128)(2,1)S(1)} %get-tuple-element.19.rest_8_), channel_id=1, source_target_pairs={{0,16},{16,0},{1,17},{17,1},{2,18},{18,2},{3,19},{19,3},{4,20},{20... | collective-permute-start | bytes 1572872 | tf_op jit(solution)/shard_map/ppermute | solution.py:527
  26.8 6.1 %collective-permute-start.8 = (bf16[4,2,32,1024]{3,2,1,0:T(8,128)(2,1)S(1)}, bf16[4,2,32,1024]{3,2,1,0:T(8,128)(2,1)S(1)}, u32[]{:S(2)}, u32[]{:S(2)}) collective-permute-start(bf16[4,2,32,1024]{3,2,1,0:T(8,128)(2,1)S(1)} %maximum_bitcast_fusion.rest_0_), channel_id=1, source_target_pairs={{0,12},{1,13},{2,14},{3,15},{4,0},{5,1},{6,2},{7,3},{8,4},{9,5},{1... | collective-permute-start | bytes 1572872 | tf_op jit(solution)/shard_map/ppermute | solution.py:146
  33.4 1.5 %collective-permute-start.11 = (bf16[1,4,2,32,1024]{4,3,2,1,0:T(8,128)(2,1)S(1)}, bf16[1,4,2,32,1024]{4,3,2,1,0:T(8,128)(2,1)}, u32[]{:S(2)}, u32[]{:S(2)}) collective-permute-start(bf16[1,4,2,32,1024]{4,3,2,1,0:T(8,128)(2,1)S(1)} %get-tuple-element.19.rest_8_), channel_id=1, source_target_pairs={{0,2},{1,3},{2,0},{3,1},{4,6},{5,7},{6,4},{7,5},{8,10},{9,11},{10,... | collective-permute-start | bytes 1572872 | tf_op jit(solution)/shard_map/ppermute | solution.py:122
  35.5 2.3 %collective-permute-done.14.rest_12_ = bf16[1,4,2,32,1024]{4,3,2,1,0:T(8,128)(2,1)} collective-permute-done((bf16[1,4,2,32,1024]{4,3,2,1,0:T(8,128)(2,1)S(1)}, bf16[1,4,2,32,1024]{4,3,2,1,0:T(8,128)(2,1)}, u32[]{:S(2)}, u32[]{:S(2)}) %collective-permute-start.14) | collective-permute-done | bytes 524320 | tf_op jit(solution)/shard_map/ppermute | solution.py:527
  37.8 9.3 %collective-permute-done.8.rest_1_ = bf16[4,2,32,1024]{3,2,1,0:T(8,128)(2,1)S(1)} collective-permute-done((bf16[4,2,32,1024]{3,2,1,0:T(8,128)(2,1)S(1)}, bf16[4,2,32,1024]{3,2,1,0:T(8,128)(2,1)S(1)}, u32[]{:S(2)}, u32[]{:S(2)}) %collective-permute-start.8) | collective-permute-done | bytes 524320 | tf_op jit(solution)/shard_map/ppermute | solution.py:146
  49.8 9.2 %collective-permute-done.11.rest_9_ = bf16[1,4,2,32,1024]{4,3,2,1,0:T(8,128)(2,1)} collective-permute-done((bf16[1,4,2,32,1024]{4,3,2,1,0:T(8,128)(2,1)S(1)}, bf16[1,4,2,32,1024]{4,3,2,1,0:T(8,128)(2,1)}, u32[]{:S(2)}, u32[]{:S(2)}) %collective-permute-start.11) | collective-permute-done | bytes 524320 | tf_op jit(solution)/shard_map/ppermute | solution.py:122
  59.1 1.7 %slice.27 = bf16[1,4,1,32,1024]{4,3,2,1,0:T(8,128)(2,1)} slice(bf16[1,4,2,32,1024]{4,3,2,1,0:T(8,128)(2,1)} %collective-permute-done.11.rest_9_), slice={[0:1], [0:4], [1:2], [0:32], [0:1024]} | slice | bytes 524288 | tf_op jit(solution)/shard_map/slice | solution.py:530
  63.8 2.2 %fusion.14 = (bf16[8,128,128]{2,1,0:T(8,128)(2,1)S(1)}, bf16[8,128,128]{2,1,0:T(8,128)(2,1)S(1)}, bf16[8,128,128]{2,1,0:T(8,128)(2,1)S(1)}) fusion(s32[8,128]{1,0:T(8,128)S(1)} %iota_add_fusion), kind=kLoop, calls=%fused_computation.45 | loop fusion | flops 2359296 | bytes 790528 | tf_op jit(solution)/shard_map/convert.11
  66.0 3.8 %collective-permute-done.17.rest_15_ = bf16[1,4,1,32,1024]{4,3,2,1,0:T(8,128)(2,1)} collective-permute-done((bf16[1,4,1,32,1024]{4,3,2,1,0:T(8,128)(2,1)}, bf16[1,4,1,32,1024]{4,3,2,1,0:T(8,128)(2,1)}, u32[]{:S(2)}, u32[]{:S(2)}) %collective-permute-start.17) | collective-permute-done | bytes 262176 | tf_op jit(solution)/shard_map/ppermute | solution.py:530
  72.3 2.0 %copy-done.1 = f32[8,512,256]{2,1,0:T(8,128)} copy-done((f32[8,512,256]{2,1,0:T(8,128)}, f32[8,512,256]{2,1,0:T(8,128)S(1)}, u32[]{:S(2)}) %copy-start.1) | copy-done | bytes 4194328
  74.3 5.0 %collective-permute-done.10.rest_3_ = bf16[4,2,32,1024]{3,2,1,0:T(8,128)(2,1)} collective-permute-done((bf16[4,2,32,1024]{3,2,1,0:T(8,128)(2,1)}, bf16[4,2,32,1024]{3,2,1,0:T(8,128)(2,1)}, u32[]{:S(2)}, u32[]{:S(2)}) %collective-permute-start.10) | collective-permute-done | bytes 524320 | tf_op jit(solution)/shard_map/ppermute | solution.py:146
  79.3 3.6 %lag_scores.1 = (bf16[512,256]{1,0:T(8,128)(2,1)S(1)}, bf16[512,256]{1,0:T(8,128)(2,1)S(1)}, bf16[512,256]{1,0:T(8,128)(2,1)S(1)}, bf16[512,256]{1,0:T(8,128)(2,1)S(1)}) custom-call(s32[2]{0:T(128)S(1)} %pad_add_fusion.where_ref, f32[2,512,1024]{2,1,0:T(8,128)S(1)} %get-tuple-element.12.spectrum, bf16[8,256,256]{2,1,0:T(8,128)(2,1)S(1)} %maximum_maximum_fusion.stage_one, ...), custom_call_target="tpu_custom_call" | custom-call | tf_op jit(solution)/shard_map/lag_scores/pallas_call | solution.py:484
  86.8 28.1 %collective-permute-done.20 = bf16[512,256]{1,0:T(8,128)(2,1)S(1)} collective-permute-done((bf16[512,256]{1,0:T(8,128)(2,1)S(1)}, bf16[512,256]{1,0:T(8,128)(2,1)S(1)}, u32[]{:S(2)}, u32[]{:S(2)}) %collective-permute-start.20) | collective-permute-done | bytes 262176 | tf_op jit(solution)/shard_map/ppermute | solution.py:559
  115.0 20.3 %collective-permute-done.21 = bf16[512,256]{1,0:T(8,128)(2,1)S(1)} collective-permute-done((bf16[512,256]{1,0:T(8,128)(2,1)S(1)}, bf16[512,256]{1,0:T(8,128)(2,1)S(1)}, u32[]{:S(2)}, u32[]{:S(2)}) %collective-permute-start.21) | collective-permute-done | bytes 262176 | tf_op jit(solution)/shard_map/ppermute | solution.py:559
  136.0 4.4 %collective-permute-done.23 = bf16[512,128]{1,0:T(8,128)(2,1)S(1)} collective-permute-done((bf16[512,128]{1,0:T(8,128)(2,1)S(1)}, bf16[512,128]{1,0:T(8,128)(2,1)S(1)}, u32[]{:S(2)}, u32[]{:S(2)}) %collective-permute-start.23) | collective-permute-done | bytes 131104 | tf_op jit(solution)/shard_map/ppermute | solution.py:567
  140.7 1.3 collective-permute-done.24
  142.7 3.8 %collective-permute-done.25 = bf16[256,64]{1,0:T(8,128)(2,1)S(1)} collective-permute-done((bf16[256,64]{1,0:T(8,128)(2,1)S(1)}, bf16[256,64]{1,0:T(8,128)(2,1)S(1)}, u32[]{:S(2)}, u32[]{:S(2)}) %collective-permute-start.25) | collective-permute-done | bytes 32800 | tf_op jit(solution)/shard_map/ppermute | solution.py:575
  (102 shorter events, 22.0 us)
Async XLA Ops:
  1.2 16.4 %collective-permute-start.6 = (bf16[1,2,2,32,1024]{4,3,2,0,1:T(8,128)(2,1)S(1)}, bf16[1,2,2,32,1024]{4,3,2,0,1:T(8,128)(2,1)S(1)}, u32[]{:S(2)}, u32[]{:S(2)}) collective-permute-start(bf16[1,2,2,32,1024]{4,3,2,0,1:T(8,128)(2,1)S(1)} %get-tuple-element.27), channel_id=1, source_target_pairs={{0,2},{1,3},{2,0},{3,1},{4,6},{5,7},{6,4},{7,5},{8,10},{9,11},{10,... | collective-permute-start | bytes 786440 | tf_op jit(solution)/shard_map/ppermute | solution.py:138
  5.0 12.7 %collective-permute-start.2 = (bf16[4,32,1024]{2,1,0:T(8,128)(2,1)S(1)}, bf16[4,32,1024]{2,1,0:T(8,128)(2,1)S(1)}, u32[]{:S(2)}, u32[]{:S(2)}) collective-permute-start(bf16[4,32,1024]{2,1,0:T(8,128)(2,1)S(1)} %get-tuple-element.22), channel_id=1, source_target_pairs={{4,0},{5,1},{6,2},{7,3},{8,4},{9,5},{10,6},{11,7},{12,8},{13,9},{1... | collective-permute-start | bytes 786440 | tf_op jit(solution)/shard_map/ppermute | solution.py:114
  7.4 12.3 %collective-permute-start = (bf16[4,32,1024]{2,1,0:T(8,128)(2,1)S(1)}, bf16[4,32,1024]{2,1,0:T(8,128)(2,1)S(1)}, u32[]{:S(2)}, u32[]{:S(2)}) collective-permute-start(bf16[4,32,1024]{2,1,0:T(8,128)(2,1)S(1)} %get-tuple-element.24), channel_id=1, source_target_pairs={{0,4},{1,5},{2,6},{3,7},{4,8},{5,9},{6,10},{7,11},{12,0},{13,1},{1... | collective-permute-start | bytes 786440 | tf_op jit(solution)/shard_map/ppermute | solution.py:114
  8.7 15.2 %collective-permute-start.1 = (bf16[4,32,1024]{2,1,0:T(8,128)(2,1)S(1)}, bf16[4,32,1024]{2,1,0:T(8,128)(2,1)}, u32[]{:S(2)}, u32[]{:S(2)}) collective-permute-start(bf16[4,32,1024]{2,1,0:T(8,128)(2,1)S(1)} %get-tuple-element.23), channel_id=1, source_target_pairs={{0,8},{1,9},{2,10},{3,11},{8,0},{9,1},{10,2},{11,3},{12,4},{13,5},... | collective-permute-start | bytes 786440 | tf_op jit(solution)/shard_map/ppermute | solution.py:114
  17.6 9.1 %collective-permute-start.7 = (bf16[2,1,2,32,1024]{4,3,2,0,1:T(8,128)(2,1)S(1)}, bf16[2,1,2,32,1024]{4,3,2,0,1:T(8,128)(2,1)S(1)}, u32[]{:S(2)}, u32[]{:S(2)}) collective-permute-start(bf16[2,1,2,32,1024]{4,3,2,0,1:T(8,128)(2,1)S(1)} %get-tuple-element.26), channel_id=1, source_target_pairs={{0,1},{1,0},{2,3},{3,2},{4,5},{5,4},{6,7},{7,6},{8,9},{9,8},{10,11... | collective-permute-start | bytes 786440 | tf_op jit(solution)/shard_map/ppermute | solution.py:138
  25.1 12.7 %collective-permute-start.14 = (bf16[1,4,2,32,1024]{4,3,2,1,0:T(8,128)(2,1)S(1)}, bf16[1,4,2,32,1024]{4,3,2,1,0:T(8,128)(2,1)}, u32[]{:S(2)}, u32[]{:S(2)}) collective-permute-start(bf16[1,4,2,32,1024]{4,3,2,1,0:T(8,128)(2,1)S(1)} %get-tuple-element.19.rest_8_), channel_id=1, source_target_pairs={{0,16},{16,0},{1,17},{17,1},{2,18},{18,2},{3,19},{19,3},{4,20},{20... | collective-permute-start | bytes 1572872 | tf_op jit(solution)/shard_map/ppermute | solution.py:527
  26.8 20.3 %collective-permute-start.8 = (bf16[4,2,32,1024]{3,2,1,0:T(8,128)(2,1)S(1)}, bf16[4,2,32,1024]{3,2,1,0:T(8,128)(2,1)S(1)}, u32[]{:S(2)}, u32[]{:S(2)}) collective-permute-start(bf16[4,2,32,1024]{3,2,1,0:T(8,128)(2,1)S(1)} %maximum_bitcast_fusion.rest_0_), channel_id=1, source_target_pairs={{0,12},{1,13},{2,14},{3,15},{4,0},{5,1},{6,2},{7,3},{8,4},{9,5},{1... | collective-permute-start | bytes 1572872 | tf_op jit(solution)/shard_map/ppermute | solution.py:146
  32.8 15.6 %collective-permute-start.3 = (bf16[1,4,2,32,1024]{4,3,2,1,0:T(8,128)(2,1)S(1)}, bf16[1,4,2,32,1024]{4,3,2,1,0:T(8,128)(2,1)S(1)}, u32[]{:S(2)}, u32[]{:S(2)}) collective-permute-start(bf16[1,4,2,32,1024]{4,3,2,1,0:T(8,128)(2,1)S(1)} %get-tuple-element.20.rest_0_.rest_4_), channel_id=1, source_target_pairs={{0,2},{1,3},{2,0},{3,1},{4,6},{5,7},{6,4},{7,5},{8,10},{9,11},{10,... | collective-permute-start | bytes 1572872 | tf_op jit(solution)/shard_map/ppermute | solution.py:122
  33.4 25.6 %collective-permute-start.11 = (bf16[1,4,2,32,1024]{4,3,2,1,0:T(8,128)(2,1)S(1)}, bf16[1,4,2,32,1024]{4,3,2,1,0:T(8,128)(2,1)}, u32[]{:S(2)}, u32[]{:S(2)}) collective-permute-start(bf16[1,4,2,32,1024]{4,3,2,1,0:T(8,128)(2,1)S(1)} %get-tuple-element.19.rest_8_), channel_id=1, source_target_pairs={{0,2},{1,3},{2,0},{3,1},{4,6},{5,7},{6,4},{7,5},{8,10},{9,11},{10,... | collective-permute-start | bytes 1572872 | tf_op jit(solution)/shard_map/ppermute | solution.py:122
  35.4 25.4 %collective-permute-start.4 = (bf16[1,4,2,32,1024]{4,3,2,1,0:T(8,128)(2,1)S(1)}, bf16[1,4,2,32,1024]{4,3,2,1,0:T(8,128)(2,1)S(1)}, u32[]{:S(2)}, u32[]{:S(2)}) collective-permute-start(bf16[1,4,2,32,1024]{4,3,2,1,0:T(8,128)(2,1)S(1)} %get-tuple-element.20.rest_0_.rest_4_), channel_id=1, source_target_pairs={{0,1},{1,0},{2,3},{3,2},{4,5},{5,4},{6,7},{7,6},{8,9},{9,8},{10,11... | collective-permute-start | bytes 1572872 | tf_op jit(solution)/shard_map/ppermute | solution.py:130
  37.8 23.5 %collective-permute-start.12 = (bf16[1,4,2,32,1024]{4,3,2,1,0:T(8,128)(2,1)S(1)}, bf16[1,4,2,32,1024]{4,3,2,1,0:T(8,128)(2,1)S(1)}, u32[]{:S(2)}, u32[]{:S(2)}) collective-permute-start(bf16[1,4,2,32,1024]{4,3,2,1,0:T(8,128)(2,1)S(1)} %get-tuple-element.19.rest_8_), channel_id=1, source_target_pairs={{0,1},{1,0},{2,3},{3,2},{4,5},{5,4},{6,7},{7,6},{8,9},{9,8},{10,11... | collective-permute-start | bytes 1572872 | tf_op jit(solution)/shard_map/ppermute | solution.py:130
  47.1 15.5 %collective-permute-start.9 = (bf16[4,2,32,1024]{3,2,1,0:T(8,128)(2,1)S(1)}, bf16[4,2,32,1024]{3,2,1,0:T(8,128)(2,1)}, u32[]{:S(2)}, u32[]{:S(2)}) collective-permute-start(bf16[4,2,32,1024]{3,2,1,0:T(8,128)(2,1)S(1)} %collective-permute-done.8.rest_1_), channel_id=1, source_target_pairs={{0,12},{1,13},{2,14},{3,15},{4,0},{5,1},{6,2},{7,3},{8,4},{9,5},{1... | collective-permute-start | bytes 1572872 | tf_op jit(solution)/shard_map/ppermute | solution.py:146
  48.4 14.1 %collective-permute-start.16 = (bf16[1,4,1,32,1024]{4,3,2,1,0:T(8,128)(2,1)S(1)}, bf16[1,4,1,32,1024]{4,3,2,1,0:T(8,128)(2,1)S(1)}, u32[]{:S(2)}, u32[]{:S(2)}) collective-permute-start(bf16[1,4,1,32,1024]{4,3,2,1,0:T(8,128)(2,1)S(1)} %slice.26), channel_id=1, source_target_pairs={{0,2},{1,3},{2,0},{3,1},{4,6},{5,7},{6,4},{7,5},{8,10},{9,11},{10,... | collective-permute-start | bytes 786440 | tf_op jit(solution)/shard_map/ppermute | solution.py:529
  59.0 10.8 %collective-permute-start.5 = (bf16[1,4,2,32,1024]{4,3,2,1,0:T(8,128)(2,1)S(1)}, bf16[1,4,2,32,1024]{4,3,2,1,0:T(8,128)(2,1)}, u32[]{:S(2)}, u32[]{:S(2)}) collective-permute-start(bf16[1,4,2,32,1024]{4,3,2,1,0:T(8,128)(2,1)S(1)} %collective-permute-done.3.rest_1_.rest_5_), channel_id=1, source_target_pairs={{0,1},{1,0},{2,3},{3,2},{4,5},{5,4},{6,7},{7,6},{8,9},{9,8},{10,11... | collective-permute-start | bytes 1572872 | tf_op jit(solution)/shard_map/ppermute | solution.py:130
  60.8 9.0 %collective-permute-start.17 = (bf16[1,4,1,32,1024]{4,3,2,1,0:T(8,128)(2,1)}, bf16[1,4,1,32,1024]{4,3,2,1,0:T(8,128)(2,1)}, u32[]{:S(2)}, u32[]{:S(2)}) collective-permute-start(bf16[1,4,1,32,1024]{4,3,2,1,0:T(8,128)(2,1)} %slice.27), channel_id=1, source_target_pairs={{0,16},{16,0},{1,17},{17,1},{2,18},{18,2},{3,19},{19,3},{4,20},{20... | collective-permute-start | bytes 786440 | tf_op jit(solution)/shard_map/ppermute | solution.py:530
  62.1 12.1 %collective-permute-start.13 = (bf16[1,4,2,32,1024]{4,3,2,1,0:T(8,128)(2,1)}, bf16[1,4,2,32,1024]{4,3,2,1,0:T(8,128)(2,1)}, u32[]{:S(2)}, u32[]{:S(2)}) collective-permute-start(bf16[1,4,2,32,1024]{4,3,2,1,0:T(8,128)(2,1)} %collective-permute-done.11.rest_9_), channel_id=1, source_target_pairs={{0,1},{1,0},{2,3},{3,2},{4,5},{5,4},{6,7},{7,6},{8,9},{9,8},{10,11... | collective-permute-start | bytes 1572872 | tf_op jit(solution)/shard_map/ppermute | solution.py:130
  62.5 11.8 %collective-permute-start.15 = (bf16[1,4,2,32,1024]{4,3,2,1,0:T(8,128)(2,1)}, bf16[1,4,2,32,1024]{4,3,2,1,0:T(8,128)(2,1)}, u32[]{:S(2)}, u32[]{:S(2)}) collective-permute-start(bf16[1,4,2,32,1024]{4,3,2,1,0:T(8,128)(2,1)} %collective-permute-done.14.rest_12_), channel_id=1, source_target_pairs={{0,1},{1,0},{2,3},{3,2},{4,5},{5,4},{6,7},{7,6},{8,9},{9,8},{10,11... | collective-permute-start | bytes 1572872 | tf_op jit(solution)/shard_map/ppermute | solution.py:130
  63.2 16.1 %collective-permute-start.10 = (bf16[4,2,32,1024]{3,2,1,0:T(8,128)(2,1)}, bf16[4,2,32,1024]{3,2,1,0:T(8,128)(2,1)}, u32[]{:S(2)}, u32[]{:S(2)}) collective-permute-start(bf16[4,2,32,1024]{3,2,1,0:T(8,128)(2,1)} %collective-permute-done.9.rest_2_), channel_id=1, source_target_pairs={{0,12},{1,13},{2,14},{3,15},{4,0},{5,1},{6,2},{7,3},{8,4},{9,5},{1... | collective-permute-start | bytes 1572872 | tf_op jit(solution)/shard_map/ppermute | solution.py:146
  69.8 4.4 %collective-permute-start.18 = (bf16[1,4,1,32,1024]{4,3,2,1,0:T(8,128)(2,1)}, bf16[1,4,1,32,1024]{4,3,2,1,0:T(8,128)(2,1)S(1)}, u32[]{:S(2)}, u32[]{:S(2)}) collective-permute-start(bf16[1,4,1,32,1024]{4,3,2,1,0:T(8,128)(2,1)} %copy-done.11), channel_id=1, source_target_pairs={{0,1},{1,0},{2,3},{3,2},{4,5},{5,4},{6,7},{7,6},{8,9},{9,8},{10,11... | collective-permute-start | bytes 786440 | tf_op jit(solution)/shard_map/ppermute | solution.py:130
  69.8 4.4 %collective-permute-start.19 = (bf16[1,4,1,32,1024]{4,3,2,1,0:T(8,128)(2,1)}, bf16[1,4,1,32,1024]{4,3,2,1,0:T(8,128)(2,1)S(1)}, u32[]{:S(2)}, u32[]{:S(2)}) collective-permute-start(bf16[1,4,1,32,1024]{4,3,2,1,0:T(8,128)(2,1)} %collective-permute-done.17.rest_15_), channel_id=1, source_target_pairs={{0,1},{1,0},{2,3},{3,2},{4,5},{5,4},{6,7},{7,6},{8,9},{9,8},{10,11... | collective-permute-start | bytes 786440 | tf_op jit(solution)/shard_map/ppermute | solution.py:130
  82.9 32.0 %collective-permute-start.20 = (bf16[512,256]{1,0:T(8,128)(2,1)S(1)}, bf16[512,256]{1,0:T(8,128)(2,1)S(1)}, u32[]{:S(2)}, u32[]{:S(2)}) collective-permute-start(bf16[512,256]{1,0:T(8,128)(2,1)S(1)} %get-tuple-element.16), channel_id=1, source_target_pairs={{0,4},{1,5},{2,6},{3,7},{4,8},{5,9},{6,10},{7,11},{8,12},{9,13},{1... | collective-permute-start | bytes 786440 | tf_op jit(solution)/shard_map/ppermute | solution.py:559
  84.2 51.0 %collective-permute-start.21 = (bf16[512,256]{1,0:T(8,128)(2,1)S(1)}, bf16[512,256]{1,0:T(8,128)(2,1)S(1)}, u32[]{:S(2)}, u32[]{:S(2)}) collective-permute-start(bf16[512,256]{1,0:T(8,128)(2,1)S(1)} %get-tuple-element.17), channel_id=1, source_target_pairs={{0,8},{1,9},{2,10},{3,11},{4,12},{5,13},{6,14},{7,15},{8,0},{9,1},... | collective-permute-start | bytes 786440 | tf_op jit(solution)/shard_map/ppermute | solution.py:559
  85.5 49.7 %collective-permute-start.22 = (bf16[512,256]{1,0:T(8,128)(2,1)S(1)}, bf16[512,256]{1,0:T(8,128)(2,1)S(1)}, u32[]{:S(2)}, u32[]{:S(2)}) collective-permute-start(bf16[512,256]{1,0:T(8,128)(2,1)S(1)} %get-tuple-element.18), channel_id=1, source_target_pairs={{0,12},{1,13},{2,14},{3,15},{4,0},{5,1},{6,2},{7,3},{8,4},{9,5},{1... | collective-permute-start | bytes 786440 | tf_op jit(solution)/shard_map/ppermute | solution.py:559
  135.4 5.0 %collective-permute-start.23 = (bf16[512,128]{1,0:T(8,128)(2,1)S(1)}, bf16[512,128]{1,0:T(8,128)(2,1)S(1)}, u32[]{:S(2)}, u32[]{:S(2)}) collective-permute-start(bf16[512,128]{1,0:T(8,128)(2,1)S(1)} %constant_dynamic-slice_fusion.2), channel_id=1, source_target_pairs={{0,2},{1,3},{2,0},{3,1},{4,6},{5,7},{6,4},{7,5},{8,10},{9,11},{10,... | collective-permute-start | bytes 393224 | tf_op jit(solution)/shard_map/ppermute | solution.py:567
  (18 other events, 236.8 us)

commit v3 on v2

--- a/solution.py
+++ b/solution.py
@@ -394,12 +394,19 @@
         variance = total(acc[0])
 
         def transforms(use):
-            def pair(cp, carry):
+            def first_stage(c0):
+                left = inner[c0].reshape(N1, 2 * PART).astype(jnp.bfloat16)
+                return jnp.dot(left, stage_one[c0], preferred_element_type=jnp.float32)
+
+            ahead = [first_stage(0), first_stage(1)]
+            for cp in range(RADIX_C // 2):
+                lags = ahead
+                if 2 * cp + 2 < RADIX_C:
+                    ahead = [first_stage(2 * cp + 2), first_stage(2 * cp + 3)]
                 columns = [[] for _ in range(RADIX_R)]
                 for half in range(2):
                     c0 = 2 * cp + half
-                    left = inner[c0].reshape(N1, 2 * PART).astype(jnp.bfloat16)
-                    lag = jnp.dot(left, stage_one[c0], preferred_element_type=jnp.float32)
+                    lag = lags[half]
                     found = [([], []) for _ in range(RADIX_R)]
                     for q in range(chunks):
                         y_re, y_im = [], []
@@ -420,9 +427,6 @@
                     right = jnp.concatenate(columns[r0], axis=1)
                     lag = jnp.dot(stage_two[r0], right, preferred_element_type=jnp.float32)
                     use(cp, r0, lag[:PART], lag[PART:])
-                return carry
-
-            lax.fori_loop(0, RADIX_C // 2, pair, 0, unroll=True)
 
         head_scale = 1.0 / (MODULUS * variance)
 
@@ -498,7 +502,7 @@
             pltpu.VMEM((plan.planes, N1, N2 // plan.planes), jnp.float32),
             pltpu.VMEM((CAL + 1, 8, N2), jnp.float32),
         ],
-        compiler_params=pltpu.CompilerParams(vmem_limit_bytes=(34 if rows % 16 == 0 else 58) * 1024 * 1024),
+        compiler_params=pltpu.CompilerParams(vmem_limit_bytes=(30 if rows % 16 == 0 else 58) * 1024 * 1024),
         name="lag_scores",
     )(where, spectrum, *tables, *streams)
 

time: 148 us -> 143 us (0.966)
  local copies, waits for them, and re-layouts: 9.33 us -> 7.36 us
  waiting for transfers between devices: 93.9 us -> 92.1 us
    ppermute x3, waiting for transfers between devices: 48.4 us -> 44.7 us  [on_device(): got = lax.ppermute(scores[o], 'freq', plan.shift_out(o))]
    unnamed x33 -> x31, local copies, waits for them, and re-layouts: 3.52 us -> 1.55 us
    ppermute x3, waiting for transfers between devices: 14.3 us -> 16.3 us  [gather_templates(): pieces.append(lax.ppermute(pieces[-1], 'freq', plan.back()))]
  transfers between devices with their start and end apart: 26 -> 26, of which waited for: 13 -> 13; matrix products, arithmetic and copies ran while one was open for 10% -> 11% of each run, Pallas kernels for 0% -> 0%
where the time goes in v3:
time: 143 us; the launch traced here: 142 us
  waiting for transfers between devices  92.1 us (64%)
  starting transfers between devices  27.6 us (19%)
  other arithmetic  11.6 us (8%)
  local copies, waits for them, and re-layouts  7.36 us (5%)
  Pallas kernels  2.93 us (2%)
    ppermute x3, waiting for transfers between devices, on_device(): got = lax.ppermute(scores[o], 'freq', plan.shift_out(o))  44.7 us
    ppermute x3, waiting for transfers between devices, gather_templates(): pieces.append(lax.ppermute(pieces[-1], 'freq', plan.back()))  16.3 us
    ppermute x2, waiting for transfers between devices, spread_plane(): got = lax.ppermute(held, 'freq', plan.swap(b))  9.22 us
    ppermute x3, starting transfers between devices, scatter_planes(): got.append(lax.ppermute(send, 'freq', plan.shift_in(o)))  8.79 us
    ppermute x3, starting transfers between devices, gather_templates(): pieces.append(lax.ppermute(pieces[-1], 'freq', plan.back()))  6.44 us
    ppermute x3, waiting for transfers between devices, scatter_planes(): got.append(lax.ppermute(send, 'freq', plan.shift_in(o)))  6.16 us
    ppermute x2, waiting for transfers between devices, on_device(): best = jnp.maximum(keep, lax.ppermute(send, 'freq', plan.swap(b)))  5.75 us
    another operation x3, other arithmetic  5.51 us
  transfers between devices with their start and end apart: 26, of which 13 were waited for; matrix products, arithmetic and copies ran while one was open for 11% of the time, Pallas kernels for 0%

profile of v3, /device:TPU:24, one launch (start us, length us, event | category | flops | bytes accessed | tf_op | source)
XLA Modules:
  0.0 142.2 jit_solution(11684091266689555454)
XLA Ops:
  1.2 1.6 %collective-permute-start.6 = (bf16[1,2,2,32,1024]{4,3,2,0,1:T(8,128)(2,1)S(1)}, bf16[1,2,2,32,1024]{4,3,2,0,1:T(8,128)(2,1)S(1)}, u32[]{:S(2)}, u32[]{:S(2)}) collective-permute-start(bf16[1,2,2,32,1024]{4,3,2,0,1:T(8,128)(2,1)S(1)} %get-tuple-element.27), channel_id=1, source_target_pairs={{0,2},{1,3},{2,0},{3,1},{4,6},{5,7},{6,4},{7,5},{8,10},{9,11},{10,... | collective-permute-start | bytes 786440 | tf_op jit(solution)/shard_map/ppermute | solution.py:138
  5.0 2.4 %collective-permute-start.2 = (bf16[4,32,1024]{2,1,0:T(8,128)(2,1)S(1)}, bf16[4,32,1024]{2,1,0:T(8,128)(2,1)S(1)}, u32[]{:S(2)}, u32[]{:S(2)}) collective-permute-start(bf16[4,32,1024]{2,1,0:T(8,128)(2,1)S(1)} %get-tuple-element.22), channel_id=1, source_target_pairs={{4,0},{5,1},{6,2},{7,3},{8,4},{9,5},{10,6},{11,7},{12,8},{13,9},{1... | collective-permute-start | bytes 786440 | tf_op jit(solution)/shard_map/ppermute | solution.py:114
  7.4 1.3 collective-permute-start
  8.7 5.1 %collective-permute-start.1 = (bf16[4,32,1024]{2,1,0:T(8,128)(2,1)S(1)}, bf16[4,32,1024]{2,1,0:T(8,128)(2,1)}, u32[]{:S(2)}, u32[]{:S(2)}) collective-permute-start(bf16[4,32,1024]{2,1,0:T(8,128)(2,1)S(1)} %get-tuple-element.23), channel_id=1, source_target_pairs={{0,8},{1,9},{2,10},{3,11},{8,0},{9,1},{10,2},{11,3},{12,4},{13,5},... | collective-permute-start | bytes 786440 | tf_op jit(solution)/shard_map/ppermute | solution.py:114
  14.3 1.4 subtract_convert_fusion
  15.7 1.9 %negate_convert_fusion.2 = (bf16[4,128,128]{2,1,0:T(8,128)(2,1)}, bf16[4,128,128]{2,1,0:T(8,128)(2,1)}, bf16[4,128,128]{2,1,0:T(8,128)(2,1)}) fusion(s32[4,128]{1,0:T(4,128)S(1)} %iota_add_fusion.1), kind=kLoop, calls=%fused_computation.37 | loop fusion | flops 1179648 | bytes 395264 | tf_op jit(solution)/shard_map/convert.5
  17.7 1.9 %collective-permute-done = bf16[4,32,1024]{2,1,0:T(8,128)(2,1)S(1)} collective-permute-done((bf16[4,32,1024]{2,1,0:T(8,128)(2,1)S(1)}, bf16[4,32,1024]{2,1,0:T(8,128)(2,1)S(1)}, u32[]{:S(2)}, u32[]{:S(2)}) %collective-permute-start) | collective-permute-done | bytes 262176 | tf_op jit(solution)/shard_map/ppermute | solution.py:114
  19.7 4.2 %collective-permute-done.1 = bf16[4,32,1024]{2,1,0:T(8,128)(2,1)} collective-permute-done((bf16[4,32,1024]{2,1,0:T(8,128)(2,1)S(1)}, bf16[4,32,1024]{2,1,0:T(8,128)(2,1)}, u32[]{:S(2)}, u32[]{:S(2)}) %collective-permute-start.1) | collective-permute-done | bytes 262176 | tf_op jit(solution)/shard_map/ppermute | solution.py:114
  25.1 1.6 %collective-permute-start.14 = (bf16[1,4,2,32,1024]{4,3,2,1,0:T(8,128)(2,1)S(1)}, bf16[1,4,2,32,1024]{4,3,2,1,0:T(8,128)(2,1)}, u32[]{:S(2)}, u32[]{:S(2)}) collective-permute-start(bf16[1,4,2,32,1024]{4,3,2,1,0:T(8,128)(2,1)S(1)} %get-tuple-element.19.rest_8_), channel_id=1, source_target_pairs={{0,16},{16,0},{1,17},{17,1},{2,18},{18,2},{3,19},{19,3},{4,20},{20... | collective-permute-start | bytes 1572872 | tf_op jit(solution)/shard_map/ppermute | solution.py:531
  26.8 6.1 %collective-permute-start.8 = (bf16[4,2,32,1024]{3,2,1,0:T(8,128)(2,1)S(1)}, bf16[4,2,32,1024]{3,2,1,0:T(8,128)(2,1)S(1)}, u32[]{:S(2)}, u32[]{:S(2)}) collective-permute-start(bf16[4,2,32,1024]{3,2,1,0:T(8,128)(2,1)S(1)} %maximum_bitcast_fusion.rest_0_), channel_id=1, source_target_pairs={{0,12},{1,13},{2,14},{3,15},{4,0},{5,1},{6,2},{7,3},{8,4},{9,5},{1... | collective-permute-start | bytes 1572872 | tf_op jit(solution)/shard_map/ppermute | solution.py:146
  33.4 1.5 %collective-permute-start.11 = (bf16[1,4,2,32,1024]{4,3,2,1,0:T(8,128)(2,1)S(1)}, bf16[1,4,2,32,1024]{4,3,2,1,0:T(8,128)(2,1)}, u32[]{:S(2)}, u32[]{:S(2)}) collective-permute-start(bf16[1,4,2,32,1024]{4,3,2,1,0:T(8,128)(2,1)S(1)} %get-tuple-element.19.rest_8_), channel_id=1, source_target_pairs={{0,2},{1,3},{2,0},{3,1},{4,6},{5,7},{6,4},{7,5},{8,10},{9,11},{10,... | collective-permute-start | bytes 1572872 | tf_op jit(solution)/shard_map/ppermute | solution.py:122
  35.5 2.3 %collective-permute-done.14.rest_12_ = bf16[1,4,2,32,1024]{4,3,2,1,0:T(8,128)(2,1)} collective-permute-done((bf16[1,4,2,32,1024]{4,3,2,1,0:T(8,128)(2,1)S(1)}, bf16[1,4,2,32,1024]{4,3,2,1,0:T(8,128)(2,1)}, u32[]{:S(2)}, u32[]{:S(2)}) %collective-permute-start.14) | collective-permute-done | bytes 524320 | tf_op jit(solution)/shard_map/ppermute | solution.py:531
  37.8 9.3 %collective-permute-done.8.rest_1_ = bf16[4,2,32,1024]{3,2,1,0:T(8,128)(2,1)S(1)} collective-permute-done((bf16[4,2,32,1024]{3,2,1,0:T(8,128)(2,1)S(1)}, bf16[4,2,32,1024]{3,2,1,0:T(8,128)(2,1)S(1)}, u32[]{:S(2)}, u32[]{:S(2)}) %collective-permute-start.8) | collective-permute-done | bytes 524320 | tf_op jit(solution)/shard_map/ppermute | solution.py:146
  49.8 9.2 %collective-permute-done.11.rest_9_ = bf16[1,4,2,32,1024]{4,3,2,1,0:T(8,128)(2,1)} collective-permute-done((bf16[1,4,2,32,1024]{4,3,2,1,0:T(8,128)(2,1)S(1)}, bf16[1,4,2,32,1024]{4,3,2,1,0:T(8,128)(2,1)}, u32[]{:S(2)}, u32[]{:S(2)}) %collective-permute-start.11) | collective-permute-done | bytes 524320 | tf_op jit(solution)/shard_map/ppermute | solution.py:122
  59.1 1.7 %slice.27 = bf16[1,4,1,32,1024]{4,3,2,1,0:T(8,128)(2,1)} slice(bf16[1,4,2,32,1024]{4,3,2,1,0:T(8,128)(2,1)} %collective-permute-done.11.rest_9_), slice={[0:1], [0:4], [1:2], [0:32], [0:1024]} | slice | bytes 524288 | tf_op jit(solution)/shard_map/slice | solution.py:534
  63.8 2.2 %fusion.14 = (bf16[8,128,128]{2,1,0:T(8,128)(2,1)S(1)}, bf16[8,128,128]{2,1,0:T(8,128)(2,1)S(1)}, bf16[8,128,128]{2,1,0:T(8,128)(2,1)S(1)}) fusion(s32[8,128]{1,0:T(8,128)S(1)} %iota_add_fusion), kind=kLoop, calls=%fused_computation.45 | loop fusion | flops 2359296 | bytes 790528 | tf_op jit(solution)/shard_map/convert.11
  66.0 3.8 %collective-permute-done.17.rest_15_ = bf16[1,4,1,32,1024]{4,3,2,1,0:T(8,128)(2,1)} collective-permute-done((bf16[1,4,1,32,1024]{4,3,2,1,0:T(8,128)(2,1)}, bf16[1,4,1,32,1024]{4,3,2,1,0:T(8,128)(2,1)}, u32[]{:S(2)}, u32[]{:S(2)}) %collective-permute-start.17) | collective-permute-done | bytes 262176 | tf_op jit(solution)/shard_map/ppermute | solution.py:534
  72.3 7.0 %collective-permute-done.10.rest_3_ = bf16[4,2,32,1024]{3,2,1,0:T(8,128)(2,1)} collective-permute-done((bf16[4,2,32,1024]{3,2,1,0:T(8,128)(2,1)}, bf16[4,2,32,1024]{3,2,1,0:T(8,128)(2,1)}, u32[]{:S(2)}, u32[]{:S(2)}) %collective-permute-start.10) | collective-permute-done | bytes 524320 | tf_op jit(solution)/shard_map/ppermute | solution.py:146
  79.3 2.3 %lag_scores.1 = (bf16[512,256]{1,0:T(8,128)(2,1)S(1)}, bf16[512,256]{1,0:T(8,128)(2,1)S(1)}, bf16[512,256]{1,0:T(8,128)(2,1)S(1)}, bf16[512,256]{1,0:T(8,128)(2,1)S(1)}) custom-call(s32[2]{0:T(128)S(1)} %pad_add_fusion.where_ref, f32[2,512,1024]{2,1,0:T(8,128)S(1)} %get-tuple-element.12.spectrum, bf16[8,256,256]{2,1,0:T(8,128)(2,1)S(1)} %maximum_maximum_fusion.stage_one, ...), custom_call_target="tpu_custom_call" | custom-call | tf_op jit(solution)/shard_map/lag_scores/pallas_call | solution.py:488
  85.6 24.4 %collective-permute-done.20 = bf16[512,256]{1,0:T(8,128)(2,1)S(1)} collective-permute-done((bf16[512,256]{1,0:T(8,128)(2,1)S(1)}, bf16[512,256]{1,0:T(8,128)(2,1)S(1)}, u32[]{:S(2)}, u32[]{:S(2)}) %collective-permute-start.20) | collective-permute-done | bytes 262176 | tf_op jit(solution)/shard_map/ppermute | solution.py:563
  110.0 20.2 %collective-permute-done.21 = bf16[512,256]{1,0:T(8,128)(2,1)S(1)} collective-permute-done((bf16[512,256]{1,0:T(8,128)(2,1)S(1)}, bf16[512,256]{1,0:T(8,128)(2,1)S(1)}, u32[]{:S(2)}, u32[]{:S(2)}) %collective-permute-start.21) | collective-permute-done | bytes 262176 | tf_op jit(solution)/shard_map/ppermute | solution.py:563
  131.0 4.4 %collective-permute-done.23 = bf16[512,128]{1,0:T(8,128)(2,1)S(1)} collective-permute-done((bf16[512,128]{1,0:T(8,128)(2,1)S(1)}, bf16[512,128]{1,0:T(8,128)(2,1)S(1)}, u32[]{:S(2)}, u32[]{:S(2)}) %collective-permute-start.23) | collective-permute-done | bytes 131104 | tf_op jit(solution)/shard_map/ppermute | solution.py:571
  135.7 1.3 collective-permute-done.24
  137.7 3.8 %collective-permute-done.25 = bf16[256,64]{1,0:T(8,128)(2,1)S(1)} collective-permute-done((bf16[256,64]{1,0:T(8,128)(2,1)S(1)}, bf16[256,64]{1,0:T(8,128)(2,1)S(1)}, u32[]{:S(2)}, u32[]{:S(2)}) %collective-permute-start.25) | collective-permute-done | bytes 32800 | tf_op jit(solution)/shard_map/ppermute | solution.py:579
  (100 shorter events, 20.7 us)
Async XLA Ops:
  1.2 16.4 %collective-permute-start.6 = (bf16[1,2,2,32,1024]{4,3,2,0,1:T(8,128)(2,1)S(1)}, bf16[1,2,2,32,1024]{4,3,2,0,1:T(8,128)(2,1)S(1)}, u32[]{:S(2)}, u32[]{:S(2)}) collective-permute-start(bf16[1,2,2,32,1024]{4,3,2,0,1:T(8,128)(2,1)S(1)} %get-tuple-element.27), channel_id=1, source_target_pairs={{0,2},{1,3},{2,0},{3,1},{4,6},{5,7},{6,4},{7,5},{8,10},{9,11},{10,... | collective-permute-start | bytes 786440 | tf_op jit(solution)/shard_map/ppermute | solution.py:138
  5.0 12.7 %collective-permute-start.2 = (bf16[4,32,1024]{2,1,0:T(8,128)(2,1)S(1)}, bf16[4,32,1024]{2,1,0:T(8,128)(2,1)S(1)}, u32[]{:S(2)}, u32[]{:S(2)}) collective-permute-start(bf16[4,32,1024]{2,1,0:T(8,128)(2,1)S(1)} %get-tuple-element.22), channel_id=1, source_target_pairs={{4,0},{5,1},{6,2},{7,3},{8,4},{9,5},{10,6},{11,7},{12,8},{13,9},{1... | collective-permute-start | bytes 786440 | tf_op jit(solution)/shard_map/ppermute | solution.py:114
  7.4 12.3 %collective-permute-start = (bf16[4,32,1024]{2,1,0:T(8,128)(2,1)S(1)}, bf16[4,32,1024]{2,1,0:T(8,128)(2,1)S(1)}, u32[]{:S(2)}, u32[]{:S(2)}) collective-permute-start(bf16[4,32,1024]{2,1,0:T(8,128)(2,1)S(1)} %get-tuple-element.24), channel_id=1, source_target_pairs={{0,4},{1,5},{2,6},{3,7},{4,8},{5,9},{6,10},{7,11},{12,0},{13,1},{1... | collective-permute-start | bytes 786440 | tf_op jit(solution)/shard_map/ppermute | solution.py:114
  8.7 15.2 %collective-permute-start.1 = (bf16[4,32,1024]{2,1,0:T(8,128)(2,1)S(1)}, bf16[4,32,1024]{2,1,0:T(8,128)(2,1)}, u32[]{:S(2)}, u32[]{:S(2)}) collective-permute-start(bf16[4,32,1024]{2,1,0:T(8,128)(2,1)S(1)} %get-tuple-element.23), channel_id=1, source_target_pairs={{0,8},{1,9},{2,10},{3,11},{8,0},{9,1},{10,2},{11,3},{12,4},{13,5},... | collective-permute-start | bytes 786440 | tf_op jit(solution)/shard_map/ppermute | solution.py:114
  17.7 9.0 %collective-permute-start.7 = (bf16[2,1,2,32,1024]{4,3,2,0,1:T(8,128)(2,1)S(1)}, bf16[2,1,2,32,1024]{4,3,2,0,1:T(8,128)(2,1)S(1)}, u32[]{:S(2)}, u32[]{:S(2)}) collective-permute-start(bf16[2,1,2,32,1024]{4,3,2,0,1:T(8,128)(2,1)S(1)} %get-tuple-element.26), channel_id=1, source_target_pairs={{0,1},{1,0},{2,3},{3,2},{4,5},{5,4},{6,7},{7,6},{8,9},{9,8},{10,11... | collective-permute-start | bytes 786440 | tf_op jit(solution)/shard_map/ppermute | solution.py:138
  25.1 12.7 %collective-permute-start.14 = (bf16[1,4,2,32,1024]{4,3,2,1,0:T(8,128)(2,1)S(1)}, bf16[1,4,2,32,1024]{4,3,2,1,0:T(8,128)(2,1)}, u32[]{:S(2)}, u32[]{:S(2)}) collective-permute-start(bf16[1,4,2,32,1024]{4,3,2,1,0:T(8,128)(2,1)S(1)} %get-tuple-element.19.rest_8_), channel_id=1, source_target_pairs={{0,16},{16,0},{1,17},{17,1},{2,18},{18,2},{3,19},{19,3},{4,20},{20... | collective-permute-start | bytes 1572872 | tf_op jit(solution)/shard_map/ppermute | solution.py:531
  26.8 20.3 %collective-permute-start.8 = (bf16[4,2,32,1024]{3,2,1,0:T(8,128)(2,1)S(1)}, bf16[4,2,32,1024]{3,2,1,0:T(8,128)(2,1)S(1)}, u32[]{:S(2)}, u32[]{:S(2)}) collective-permute-start(bf16[4,2,32,1024]{3,2,1,0:T(8,128)(2,1)S(1)} %maximum_bitcast_fusion.rest_0_), channel_id=1, source_target_pairs={{0,12},{1,13},{2,14},{3,15},{4,0},{5,1},{6,2},{7,3},{8,4},{9,5},{1... | collective-permute-start | bytes 1572872 | tf_op jit(solution)/shard_map/ppermute | solution.py:146
  32.8 15.6 %collective-permute-start.3 = (bf16[1,4,2,32,1024]{4,3,2,1,0:T(8,128)(2,1)S(1)}, bf16[1,4,2,32,1024]{4,3,2,1,0:T(8,128)(2,1)S(1)}, u32[]{:S(2)}, u32[]{:S(2)}) collective-permute-start(bf16[1,4,2,32,1024]{4,3,2,1,0:T(8,128)(2,1)S(1)} %get-tuple-element.20.rest_0_.rest_4_), channel_id=1, source_target_pairs={{0,2},{1,3},{2,0},{3,1},{4,6},{5,7},{6,4},{7,5},{8,10},{9,11},{10,... | collective-permute-start | bytes 1572872 | tf_op jit(solution)/shard_map/ppermute | solution.py:122
  33.4 25.6 %collective-permute-start.11 = (bf16[1,4,2,32,1024]{4,3,2,1,0:T(8,128)(2,1)S(1)}, bf16[1,4,2,32,1024]{4,3,2,1,0:T(8,128)(2,1)}, u32[]{:S(2)}, u32[]{:S(2)}) collective-permute-start(bf16[1,4,2,32,1024]{4,3,2,1,0:T(8,128)(2,1)S(1)} %get-tuple-element.19.rest_8_), channel_id=1, source_target_pairs={{0,2},{1,3},{2,0},{3,1},{4,6},{5,7},{6,4},{7,5},{8,10},{9,11},{10,... | collective-permute-start | bytes 1572872 | tf_op jit(solution)/shard_map/ppermute | solution.py:122
  35.4 25.4 %collective-permute-start.4 = (bf16[1,4,2,32,1024]{4,3,2,1,0:T(8,128)(2,1)S(1)}, bf16[1,4,2,32,1024]{4,3,2,1,0:T(8,128)(2,1)S(1)}, u32[]{:S(2)}, u32[]{:S(2)}) collective-permute-start(bf16[1,4,2,32,1024]{4,3,2,1,0:T(8,128)(2,1)S(1)} %get-tuple-element.20.rest_0_.rest_4_), channel_id=1, source_target_pairs={{0,1},{1,0},{2,3},{3,2},{4,5},{5,4},{6,7},{7,6},{8,9},{9,8},{10,11... | collective-permute-start | bytes 1572872 | tf_op jit(solution)/shard_map/ppermute | solution.py:130
  37.8 23.5 %collective-permute-start.12 = (bf16[1,4,2,32,1024]{4,3,2,1,0:T(8,128)(2,1)S(1)}, bf16[1,4,2,32,1024]{4,3,2,1,0:T(8,128)(2,1)S(1)}, u32[]{:S(2)}, u32[]{:S(2)}) collective-permute-start(bf16[1,4,2,32,1024]{4,3,2,1,0:T(8,128)(2,1)S(1)} %get-tuple-element.19.rest_8_), channel_id=1, source_target_pairs={{0,1},{1,0},{2,3},{3,2},{4,5},{5,4},{6,7},{7,6},{8,9},{9,8},{10,11... | collective-permute-start | bytes 1572872 | tf_op jit(solution)/shard_map/ppermute | solution.py:130
  47.1 15.5 %collective-permute-start.9 = (bf16[4,2,32,1024]{3,2,1,0:T(8,128)(2,1)S(1)}, bf16[4,2,32,1024]{3,2,1,0:T(8,128)(2,1)}, u32[]{:S(2)}, u32[]{:S(2)}) collective-permute-start(bf16[4,2,32,1024]{3,2,1,0:T(8,128)(2,1)S(1)} %collective-permute-done.8.rest_1_), channel_id=1, source_target_pairs={{0,12},{1,13},{2,14},{3,15},{4,0},{5,1},{6,2},{7,3},{8,4},{9,5},{1... | collective-permute-start | bytes 1572872 | tf_op jit(solution)/shard_map/ppermute | solution.py:146
  48.4 14.1 %collective-permute-start.16 = (bf16[1,4,1,32,1024]{4,3,2,1,0:T(8,128)(2,1)S(1)}, bf16[1,4,1,32,1024]{4,3,2,1,0:T(8,128)(2,1)S(1)}, u32[]{:S(2)}, u32[]{:S(2)}) collective-permute-start(bf16[1,4,1,32,1024]{4,3,2,1,0:T(8,128)(2,1)S(1)} %slice.26), channel_id=1, source_target_pairs={{0,2},{1,3},{2,0},{3,1},{4,6},{5,7},{6,4},{7,5},{8,10},{9,11},{10,... | collective-permute-start | bytes 786440 | tf_op jit(solution)/shard_map/ppermute | solution.py:533
  59.0 10.8 %collective-permute-start.5 = (bf16[1,4,2,32,1024]{4,3,2,1,0:T(8,128)(2,1)S(1)}, bf16[1,4,2,32,1024]{4,3,2,1,0:T(8,128)(2,1)}, u32[]{:S(2)}, u32[]{:S(2)}) collective-permute-start(bf16[1,4,2,32,1024]{4,3,2,1,0:T(8,128)(2,1)S(1)} %collective-permute-done.3.rest_1_.rest_5_), channel_id=1, source_target_pairs={{0,1},{1,0},{2,3},{3,2},{4,5},{5,4},{6,7},{7,6},{8,9},{9,8},{10,11... | collective-permute-start | bytes 1572872 | tf_op jit(solution)/shard_map/ppermute | solution.py:130
  60.8 9.0 %collective-permute-start.17 = (bf16[1,4,1,32,1024]{4,3,2,1,0:T(8,128)(2,1)}, bf16[1,4,1,32,1024]{4,3,2,1,0:T(8,128)(2,1)}, u32[]{:S(2)}, u32[]{:S(2)}) collective-permute-start(bf16[1,4,1,32,1024]{4,3,2,1,0:T(8,128)(2,1)} %slice.27), channel_id=1, source_target_pairs={{0,16},{16,0},{1,17},{17,1},{2,18},{18,2},{3,19},{19,3},{4,20},{20... | collective-permute-start | bytes 786440 | tf_op jit(solution)/shard_map/ppermute | solution.py:534
  62.1 10.2 %collective-permute-start.13 = (bf16[1,4,2,32,1024]{4,3,2,1,0:T(8,128)(2,1)}, bf16[1,4,2,32,1024]{4,3,2,1,0:T(8,128)(2,1)}, u32[]{:S(2)}, u32[]{:S(2)}) collective-permute-start(bf16[1,4,2,32,1024]{4,3,2,1,0:T(8,128)(2,1)} %collective-permute-done.11.rest_9_), channel_id=1, source_target_pairs={{0,1},{1,0},{2,3},{3,2},{4,5},{5,4},{6,7},{7,6},{8,9},{9,8},{10,11... | collective-permute-start | bytes 1572872 | tf_op jit(solution)/shard_map/ppermute | solution.py:130
  62.5 9.8 %collective-permute-start.15 = (bf16[1,4,2,32,1024]{4,3,2,1,0:T(8,128)(2,1)}, bf16[1,4,2,32,1024]{4,3,2,1,0:T(8,128)(2,1)}, u32[]{:S(2)}, u32[]{:S(2)}) collective-permute-start(bf16[1,4,2,32,1024]{4,3,2,1,0:T(8,128)(2,1)} %collective-permute-done.14.rest_12_), channel_id=1, source_target_pairs={{0,1},{1,0},{2,3},{3,2},{4,5},{5,4},{6,7},{7,6},{8,9},{9,8},{10,11... | collective-permute-start | bytes 1572872 | tf_op jit(solution)/shard_map/ppermute | solution.py:130
  63.2 16.1 %collective-permute-start.10 = (bf16[4,2,32,1024]{3,2,1,0:T(8,128)(2,1)}, bf16[4,2,32,1024]{3,2,1,0:T(8,128)(2,1)}, u32[]{:S(2)}, u32[]{:S(2)}) collective-permute-start(bf16[4,2,32,1024]{3,2,1,0:T(8,128)(2,1)} %collective-permute-done.9.rest_2_), channel_id=1, source_target_pairs={{0,12},{1,13},{2,14},{3,15},{4,0},{5,1},{6,2},{7,3},{8,4},{9,5},{1... | collective-permute-start | bytes 1572872 | tf_op jit(solution)/shard_map/ppermute | solution.py:146
  69.8 2.5 %collective-permute-start.19 = (bf16[1,4,1,32,1024]{4,3,2,1,0:T(8,128)(2,1)}, bf16[1,4,1,32,1024]{4,3,2,1,0:T(8,128)(2,1)S(1)}, u32[]{:S(2)}, u32[]{:S(2)}) collective-permute-start(bf16[1,4,1,32,1024]{4,3,2,1,0:T(8,128)(2,1)} %collective-permute-done.17.rest_15_), channel_id=1, source_target_pairs={{0,1},{1,0},{2,3},{3,2},{4,5},{5,4},{6,7},{7,6},{8,9},{9,8},{10,11... | collective-permute-start | bytes 786440 | tf_op jit(solution)/shard_map/ppermute | solution.py:130
  81.7 28.3 %collective-permute-start.20 = (bf16[512,256]{1,0:T(8,128)(2,1)S(1)}, bf16[512,256]{1,0:T(8,128)(2,1)S(1)}, u32[]{:S(2)}, u32[]{:S(2)}) collective-permute-start(bf16[512,256]{1,0:T(8,128)(2,1)S(1)} %get-tuple-element.16), channel_id=1, source_target_pairs={{0,4},{1,5},{2,6},{3,7},{4,8},{5,9},{6,10},{7,11},{8,12},{9,13},{1... | collective-permute-start | bytes 786440 | tf_op jit(solution)/shard_map/ppermute | solution.py:563
  83.0 47.3 %collective-permute-start.21 = (bf16[512,256]{1,0:T(8,128)(2,1)S(1)}, bf16[512,256]{1,0:T(8,128)(2,1)S(1)}, u32[]{:S(2)}, u32[]{:S(2)}) collective-permute-start(bf16[512,256]{1,0:T(8,128)(2,1)S(1)} %get-tuple-element.17), channel_id=1, source_target_pairs={{0,8},{1,9},{2,10},{3,11},{4,12},{5,13},{6,14},{7,15},{8,0},{9,1},... | collective-permute-start | bytes 786440 | tf_op jit(solution)/shard_map/ppermute | solution.py:563
  84.3 46.0 %collective-permute-start.22 = (bf16[512,256]{1,0:T(8,128)(2,1)S(1)}, bf16[512,256]{1,0:T(8,128)(2,1)S(1)}, u32[]{:S(2)}, u32[]{:S(2)}) collective-permute-start(bf16[512,256]{1,0:T(8,128)(2,1)S(1)} %get-tuple-element.18), channel_id=1, source_target_pairs={{0,12},{1,13},{2,14},{3,15},{4,0},{5,1},{6,2},{7,3},{8,4},{9,5},{1... | collective-permute-start | bytes 786440 | tf_op jit(solution)/shard_map/ppermute | solution.py:563
  130.4 5.0 %collective-permute-start.23 = (bf16[512,128]{1,0:T(8,128)(2,1)S(1)}, bf16[512,128]{1,0:T(8,128)(2,1)S(1)}, u32[]{:S(2)}, u32[]{:S(2)}) collective-permute-start(bf16[512,128]{1,0:T(8,128)(2,1)S(1)} %constant_dynamic-slice_fusion.2), channel_id=1, source_target_pairs={{0,2},{1,3},{2,0},{3,1},{4,6},{5,7},{6,4},{7,5},{8,10},{9,11},{10,... | collective-permute-start | bytes 393224 | tf_op jit(solution)/shard_map/ppermute | solution.py:571
  137.1 4.3 %collective-permute-start.25 = (bf16[256,64]{1,0:T(8,128)(2,1)S(1)}, bf16[256,64]{1,0:T(8,128)(2,1)S(1)}, u32[]{:S(2)}, u32[]{:S(2)}) collective-permute-start(bf16[256,64]{1,0:T(8,128)(2,1)S(1)} %constant_dynamic-slice_fusion), channel_id=1, source_target_pairs={{0,16},{16,0},{1,17},{17,1},{2,18},{18,2},{3,19},{19,3},{4,20},{20... | collective-permute-start | bytes 98312 | tf_op jit(solution)/shard_map/ppermute | solution.py:579
  (17 other events, 232.9 us)
